TPU v7x, 128 devices: a whole 4x4x4 slice. The times are simulated.
128 devices in a mesh: ctx: 16 (over z_hi, y, core), fsdp: 8 (over z_lo, x).
Axes of the slice: x: 4, y: 4, z: 4 (z_hi: 2, z_lo: 2; z = z_hi * 2 + z_lo), core: 2. Of those that a mesh axis runs over, the one named last changes fastest.
Arguments:
- tokens: bfloat16 [8, 4096, 3072], P('fsdp', 'ctx'), may hold values from -6 to 6
- norm_gain: float32 [3072], replicated, may hold values from 0.1 to 1.9
- qkv_weight: bfloat16 [3072, 2560], P('fsdp'), may hold values from -4 to 4
- block_mask: int32 [32, 32], replicated, may hold values from 0 to 1, as said below
- out_grad: bfloat16 [8, 4096, 1536], P('fsdp', 'ctx'), may hold values from -6 to 6
Outputs:
- attended: bfloat16 [8, 4096, 1536], P('fsdp', 'ctx')
- token_grad: bfloat16 [8, 4096, 3072], P('fsdp', 'ctx')
Inputs may be any that keep to these rules, and one draw needn't show every extreme that they name: `block_mask`: every block row has ones on its diagonal and beside it where those blocks exist; exactly one block row is all ones and its block column is all ones too; every other block row has at most 6 ones.
All inputs are finite; a program needn't handle non-finite values.
Results may differ from a plain program's by a relative error of at most 0.019.
Values may be sent and summed in bfloat16 or wider, within the bound.
A program may use at most 128 MiB of HBM per device.

v0:
```python
import math

import jax
import jax.numpy as jnp
from jax import lax
from jax.sharding import PartitionSpec as P

HEADS = 12
KV_HEADS = 4
HEAD_DIM = 128
BLOCK = 128


epsilon = 1e-05
very_low = -1e30


def expand_mask(rows_mask, block_size):
    widened = jnp.repeat(rows_mask, block_size, axis=0)
    return jnp.repeat(widened, block_size, axis=1) > 0


def shard_scores(queries, key_heads, allowed, score_scale):
    scores = (
        jnp.einsum("tkgd,skd->kgts", queries, key_heads, preferred_element_type=jnp.float32)
        * score_scale
    )
    return jnp.where(allowed[None, None], scores, very_low)


def body(tokens, norm_gain, qkv_weight, block_mask, out_grad):
    rows_here = tokens.shape[1]
    group_size = HEADS // KV_HEADS
    query_width = HEADS * HEAD_DIM
    key_width = KV_HEADS * HEAD_DIM
    score_scale = 1.0 / math.sqrt(HEAD_DIM)
    cycle_size = lax.axis_size("ctx")
    position = lax.axis_index("ctx")
    blocks_here = rows_here // BLOCK
    inputs = tokens[0].astype(jnp.float32)
    inv_rms = lax.rsqrt(jnp.mean(inputs * inputs, axis=1, keepdims=True) + epsilon)
    normed = (inputs * inv_rms * norm_gain).astype(jnp.bfloat16)
    panels = lax.all_gather(qkv_weight, "fsdp", axis=0, tiled=True)
    projected = jnp.dot(normed, panels, preferred_element_type=jnp.float32).astype(jnp.bfloat16)
    queries = projected[:, :query_width].reshape(rows_here, KV_HEADS, group_size, HEAD_DIM)
    pairs_local = projected[:, query_width:]
    pairs_all = lax.all_gather(pairs_local, "ctx", axis=0, tiled=True)
    local_mask = lax.dynamic_slice_in_dim(block_mask, position * blocks_here, blocks_here, 0)

    def unpack(shard_id):
        key_rows = lax.dynamic_slice_in_dim(pairs_all, shard_id * rows_here, rows_here, 0)
        key_heads = key_rows[:, :key_width].reshape(rows_here, KV_HEADS, HEAD_DIM)
        values = key_rows[:, key_width:].reshape(rows_here, KV_HEADS, HEAD_DIM)
        allowed = expand_mask(
            lax.dynamic_slice_in_dim(local_mask, shard_id * blocks_here, blocks_here, 1), BLOCK
        )
        return (key_heads, values, allowed)

    def forward_step(shard_id, carried):
        key_heads, values, allowed = unpack(shard_id)

        def attend(run_state):
            run_max, run_sum, run_acc = run_state
            scores = shard_scores(queries, key_heads, allowed, score_scale)
            new_max = jnp.maximum(run_max, jnp.max(scores, axis=-1))
            factor = jnp.exp(run_max - new_max)
            exp_weights = jnp.where(allowed[None, None], jnp.exp(scores - new_max[..., None]), 0.0)
            run_sum = run_sum * factor + jnp.sum(exp_weights, axis=-1)
            run_acc = run_acc * factor[..., None] + jnp.einsum(
                "kgts,skd->kgtd",
                exp_weights.astype(jnp.bfloat16),
                values,
                preferred_element_type=jnp.float32,
            )
            return (new_max, run_sum, run_acc)

        return lax.cond(jnp.any(allowed), attend, lambda run_state: run_state, carried)

    initial = (
        jnp.full((KV_HEADS, group_size, rows_here), very_low, jnp.float32),
        jnp.zeros((KV_HEADS, group_size, rows_here), jnp.float32),
        jnp.zeros((KV_HEADS, group_size, rows_here, HEAD_DIM), jnp.float32),
    )
    run_max, run_sum, run_acc = lax.fori_loop(0, cycle_size, forward_step, initial)
    safe_sum = jnp.where(run_sum > 0, run_sum, 1.0)
    log_total = run_max + jnp.log(safe_sum)
    attended = (
        (run_acc / safe_sum[..., None])
        .transpose(2, 0, 1, 3)
        .reshape(rows_here, query_width)
        .astype(jnp.bfloat16)
    )
    grads_half = out_grad[0]
    grad_heads = grads_half.reshape(rows_here, KV_HEADS, group_size, HEAD_DIM)
    attended_heads = attended.astype(jnp.float32).reshape(rows_here, KV_HEADS, group_size, HEAD_DIM)
    delta_rows = jnp.sum(grad_heads.astype(jnp.float32) * attended_heads, axis=-1).transpose(
        1, 2, 0
    )

    def grad_shard(shard_id, query_grad):
        key_heads, values, allowed = unpack(shard_id)

        def compute(grad_state):
            scores = shard_scores(queries, key_heads, allowed, score_scale)
            prob_full = jnp.where(allowed[None, None], jnp.exp(scores - log_total[..., None]), 0.0)
            value_grad = jnp.einsum(
                "kgts,tkgd->skd",
                prob_full.astype(jnp.bfloat16),
                grad_heads,
                preferred_element_type=jnp.float32,
            )
            prob_grad = jnp.einsum(
                "tkgd,skd->kgts", grad_heads, values, preferred_element_type=jnp.float32
            )
            score_half = (prob_full * (prob_grad - delta_rows[..., None])).astype(jnp.bfloat16)
            grad_state = (
                grad_state
                + jnp.einsum(
                    "kgts,skd->kgtd", score_half, key_heads, preferred_element_type=jnp.float32
                )
                * score_scale
            )
            key_grad = (
                jnp.einsum(
                    "kgts,tkgd->skd", score_half, queries, preferred_element_type=jnp.float32
                )
                * score_scale
            )
            block_grads = jnp.concatenate(
                [key_grad.reshape(rows_here, key_width), value_grad.reshape(rows_here, key_width)],
                axis=1,
            )
            return (grad_state, block_grads)

        def ignore(grad_state):
            return (grad_state, jnp.zeros((rows_here, 2 * key_width), jnp.float32))

        return lax.cond(jnp.any(allowed), compute, ignore, query_grad)

    query_zero = jnp.zeros((KV_HEADS, group_size, rows_here, HEAD_DIM), jnp.float32)

    def whole_step(shard_id, carried):
        query_grad, block_terms = carried
        query_grad, block_grads = grad_shard(shard_id, query_grad)
        return (
            query_grad,
            lax.dynamic_update_slice_in_dim(block_terms, block_grads, shard_id * rows_here, 0),
        )

    empty_terms = jnp.zeros((cycle_size * rows_here, 2 * key_width), jnp.float32)
    query_grad, block_terms = lax.fori_loop(0, cycle_size, whole_step, (query_zero, empty_terms))
    pair_grads = lax.psum_scatter(
        block_terms.astype(jnp.bfloat16), "ctx", scatter_dimension=0, tiled=True
    ).astype(jnp.float32)
    query_rows_grad = query_grad.transpose(2, 0, 1, 3).reshape(rows_here, query_width)
    projected_grad = jnp.concatenate([query_rows_grad, pair_grads], axis=1).astype(jnp.bfloat16)
    normed_grad = lax.dot_general(
        projected_grad, panels, (((1,), (1,)), ((), ())), preferred_element_type=jnp.float32
    )
    scaled = normed_grad * norm_gain
    token_grad = inv_rms * scaled - inputs * inv_rms**3 * jnp.mean(
        scaled * inputs, axis=1, keepdims=True
    )
    return (attended[None], token_grad.astype(jnp.bfloat16)[None])


def solution(mesh):
    in_specs = (P("fsdp", "ctx", None), P(), P("fsdp", None), P(), P("fsdp", "ctx", None))
    out_specs = (P("fsdp", "ctx", None), P("fsdp", "ctx", None))
    return jax.shard_map(body, mesh=mesh, in_specs=in_specs, out_specs=out_specs, check_vma=False)
```

profile of v0, /device:TPU:0, one launch (start us, length us, event | category | flops | bytes accessed | tf_op | source)
XLA Modules:
  0.0 678.9 jit_solution(12386598298918545160)
XLA Ops:
  9.8 163.2 %all-gather.3.cloned.1.call-done = bf16[3072,2560]{1,0:T(8,128)(2,1)} async-done(((bf16[384,2560]{1,0:T(8,128)(2,1)}), bf16[3072,2560]{1,0:T(8,128)(2,1)}) %all-gather.3.cloned.1.call-update) | async-done | bytes 15728656 | tf_op jit(solution)/shard_map/all_gather | solution.py:43
  173.0 8.1 %convolution_convert_fusion = bf16[256,2560]{1,0:T(8,128)(2,1)S(1)} fusion(bf16[3072,2560]{1,0:T(8,128)(2,1)} %all-gather.3.cloned.1.call-done, bf16[1,256,3072]{2,1,0:T(8,128)(2,1)S(1)} %copy-done.4, f32[3072]{0:T(1024)S(1)} %copy-done.9, f32[256]{0:T(256)S(1)} %get-tuple-element.540), kind=kOutput, calls=%fused_computation.54 | convolution fusion | flops 4030332928 | bytes 18625536 | tf_op jit(solution)/shard_map/dot_general | solution.py:44
  185.2 69.5 %all-gather.5.cloned.1.call-done = bf16[4096,1024]{1,0:T(8,128)(2,1)} async-done(((bf16[256,1024]{1,0:T(8,128)(2,1)}), bf16[4096,1024]{1,0:T(8,128)(2,1)}) %all-gather.5.cloned.1.call-update) | async-done | bytes 8388624 | tf_op jit(solution)/shard_map/all_gather | solution.py:47
  254.7 11.3 %copy.57 = bf16[4096,1024]{0,1:T(8,128)(2,1)} copy(bf16[4096,1024]{1,0:T(8,128)(2,1)} %all-gather.5.cloned.1.call-done) | data formatting | bytes 16777216 | tf_op jit(solution)/shard_map/while | solution.py:84
  267.3 59.1 %while.35 = (s32[]{:T(128)}, f32[4,3,256]{2,1,0:T(4,128)S(1)}, f32[4,3,256]{2,1,0:T(4,128)S(1)}, f32[4,3,256,128]{3,2,1,0:T(8,128)}, s32[2,32]{0,1:T(8,128)S(1)}...) while((s32[]{:T(128)}, f32[4,3,256]{2,1,0:T(4,128)S(1)}, ...), condition=%wide.region_7.8_spmd, body=%wide.region_1.7_spmd.sunk | while | flops 413735936 | bytes 27996616 | solution.py:84
  269.0 5.4 conditional.4
  276.0 5.4 conditional.4
  284.7 5.4 conditional.4
  296.8 5.4 conditional.4
  303.8 5.4 conditional.4
  316.0 5.4 conditional.4
  328.3 2.3 multiply_reduce_fusion
  330.8 4.4 broadcast_in_dim.107
  335.1 86.9 %while.36 = (s32[]{:T(128)}, f32[4,3,256,128]{3,2,1,0:T(8,128)S(1)}, bf16[4096,1024]{0,1:T(8,128)(2,1)}, s32[2,32]{0,1:T(8,128)S(1)}, bf16[4096,1024]{0,1:T(8,12...) while((s32[]{:T(128)}, ...), condition=%wide.region_13.14_spmd, body=%wide.region_9.13_spmd.sunk | while | flops 1018233856 | bytes 25150352 | solution.py:151
  336.5 8.2 %conditional.5 = (f32[4,3,256,128]{3,2,1,0:T(8,128)S(1)}, bf16[256,1024]{0,1:T(8,128)(2,1)S(1)}) conditional(s32[]{:T(128)} %convert_element_type.105, f32[4,3,256,128]{3,2,1,0:T(8,128)S(1)} %get-tuple-element.710, (s32[256,2]{0,1:T(2,128)S(1)}, bf16[4096,1024]{0,1:T(8,128)(2,1)}, s32[]{:T(128)}, bf16[256,4,3,128]{0,3,2,1:T(8,128)(2,1)S(1)}, ...), branch_computations={%region_11.11_spmd, %region_12.12_spmd} | conditional | flops 1018167808 | bytes 24091684 | solution.py:138
  340.4 2.3 fusion.16
  347.1 8.2 %conditional.5 = (f32[4,3,256,128]{3,2,1,0:T(8,128)S(1)}, bf16[256,1024]{0,1:T(8,128)(2,1)S(1)}) conditional(s32[]{:T(128)} %convert_element_type.105, f32[4,3,256,128]{3,2,1,0:T(8,128)S(1)} %get-tuple-element.710, (s32[256,2]{0,1:T(2,128)S(1)}, bf16[4096,1024]{0,1:T(8,128)(2,1)}, s32[]{:T(128)}, bf16[256,4,3,128]{0,3,2,1:T(8,128)(2,1)S(1)}, ...), branch_computations={%region_11.11_spmd, %region_12.12_spmd} | conditional | flops 1018167808 | bytes 24091684 | solution.py:138
  348.8 2.1 fusion.21
  350.9 2.3 fusion.16
  359.9 8.2 %conditional.5 = (f32[4,3,256,128]{3,2,1,0:T(8,128)S(1)}, bf16[256,1024]{0,1:T(8,128)(2,1)S(1)}) conditional(s32[]{:T(128)} %convert_element_type.105, f32[4,3,256,128]{3,2,1,0:T(8,128)S(1)} %get-tuple-element.710, (s32[256,2]{0,1:T(2,128)S(1)}, bf16[4096,1024]{0,1:T(8,128)(2,1)}, s32[]{:T(128)}, bf16[256,4,3,128]{0,3,2,1:T(8,128)(2,1)S(1)}, ...), branch_computations={%region_11.11_spmd, %region_12.12_spmd} | conditional | flops 1018167808 | bytes 24091684 | solution.py:138
  363.8 2.3 fusion.16
  377.6 8.2 %conditional.5 = (f32[4,3,256,128]{3,2,1,0:T(8,128)S(1)}, bf16[256,1024]{0,1:T(8,128)(2,1)S(1)}) conditional(s32[]{:T(128)} %convert_element_type.105, f32[4,3,256,128]{3,2,1,0:T(8,128)S(1)} %get-tuple-element.710, (s32[256,2]{0,1:T(2,128)S(1)}, bf16[4096,1024]{0,1:T(8,128)(2,1)}, s32[]{:T(128)}, bf16[256,4,3,128]{0,3,2,1:T(8,128)(2,1)S(1)}, ...), branch_computations={%region_11.11_spmd, %region_12.12_spmd} | conditional | flops 1018167808 | bytes 24091684 | solution.py:138
  379.4 2.1 fusion.21
  381.5 2.3 fusion.16
  388.1 8.2 %conditional.5 = (f32[4,3,256,128]{3,2,1,0:T(8,128)S(1)}, bf16[256,1024]{0,1:T(8,128)(2,1)S(1)}) conditional(s32[]{:T(128)} %convert_element_type.105, f32[4,3,256,128]{3,2,1,0:T(8,128)S(1)} %get-tuple-element.710, (s32[256,2]{0,1:T(2,128)S(1)}, bf16[4096,1024]{0,1:T(8,128)(2,1)}, s32[]{:T(128)}, bf16[256,4,3,128]{0,3,2,1:T(8,128)(2,1)S(1)}, ...), branch_computations={%region_11.11_spmd, %region_12.12_spmd} | conditional | flops 1018167808 | bytes 24091684 | solution.py:138
  392.0 2.3 fusion.16
  405.8 8.2 %conditional.5 = (f32[4,3,256,128]{3,2,1,0:T(8,128)S(1)}, bf16[256,1024]{0,1:T(8,128)(2,1)S(1)}) conditional(s32[]{:T(128)} %convert_element_type.105, f32[4,3,256,128]{3,2,1,0:T(8,128)S(1)} %get-tuple-element.710, (s32[256,2]{0,1:T(2,128)S(1)}, bf16[4096,1024]{0,1:T(8,128)(2,1)}, s32[]{:T(128)}, bf16[256,4,3,128]{0,3,2,1:T(8,128)(2,1)S(1)}, ...), branch_computations={%region_11.11_spmd, %region_12.12_spmd} | conditional | flops 1018167808 | bytes 24091684 | solution.py:138
  407.5 2.1 fusion.21
  409.6 2.3 fusion.16
  424.6 231.6 %reduce-scatter.2.cloned.1.call-done = bf16[256,1024]{0,1:T(8,128)(2,1)} async-done(((bf16[4096,1024]{0,1:T(8,128)(2,1)}), bf16[256,1024]{0,1:T(8,128)(2,1)}) %reduce-scatter.2.cloned.1.call-update) | async-done | bytes 524304 | tf_op jit(solution)/shard_map/reduce_scatter | solution.py:152
  656.2 12.1 %fusion.34 = (f32[256]{0:T(256)S(1)}, f32[256,3072]{1,0:T(8,128)}) fusion(bf16[1,256,3072]{2,1,0:T(8,128)(2,1)} %param.13, f32[3072]{0:T(1024)S(1)} %copy-done.9, bf16[3072,2560]{1,0:T(8,128)(2,1)} %all-gather.3.cloned.1.call-done, bf16[256,1024]{0,1:T(8,128)(2,1)} %reduce-scatter.2.cloned.1.call-done, bf16[256,1536]{0,1:T(8,128)(2,1)S(1)} %bitcast.149), kind=kOutput, calls=%fused_computation.61 | convolution fusion | flops 4032298752 | bytes 21771264 | tf_op jit(solution)/shard_map/dot_general | solution.py:157
  668.3 4.0 fusion.35
  (370 shorter events, 116.5 us)
Async XLA Ops:
  7.2 176.1 %copy-start = (s32[32,32]{1,0:T(8,128)S(1)}, s32[32,32]{1,0:T(8,128)}, u32[]{:S(2)}) copy-start(s32[32,32]{1,0:T(8,128)} %param.16) | copy-start | bytes 12292
  7.2 165.8 %copy-start.4 = (bf16[1,256,3072]{2,1,0:T(8,128)(2,1)S(1)}, bf16[1,256,3072]{2,1,0:T(8,128)(2,1)}, u32[]{:S(2)}) copy-start(bf16[1,256,3072]{2,1,0:T(8,128)(2,1)} %param.13) | copy-start | bytes 4718596
  7.2 165.8 %copy-start.9 = (f32[3072]{0:T(1024)S(1)}, f32[3072]{0:T(1024)}, u32[]{:S(2)}) copy-start(f32[3072]{0:T(1024)} %param.14) | copy-start | bytes 36868
  7.2 165.7 %all-gather.3.cloned.1.call-start = ((), (), s32[]{:S(2)}) async-start(), calls=%async_computation.1 | async-start | bytes 17694720 | tf_op jit(solution)/shard_map/all_gather | solution.py:43
  7.9 246.7 %all-gather.5.cloned.1.call-start = ((), (), s32[]{:S(2)}) async-start(), calls=%async_computation.2 | async-start | bytes 8912896 | tf_op jit(solution)/shard_map/all_gather | solution.py:47
  173.0 10.4 %copy-start.8 = (bf16[1,256,1536]{2,1,0:T(8,128)(2,1)S(1)}, bf16[1,256,1536]{2,1,0:T(8,128)(2,1)}, u32[]{:S(2)}) copy-start(bf16[1,256,1536]{2,1,0:T(8,128)(2,1)} %param.17) | copy-start | bytes 2359300
  181.0 1.1 copy-start.6
  183.0 1.5 slice-start
  183.0 473.2 %reduce-scatter.2.cloned.1.call-start = ((), (), s32[]{:S(2)}) async-start(), calls=%async_computation.3 | async-start | bytes 8912896 | tf_op jit(solution)/shard_map/reduce_scatter | solution.py:152
  270.1 1.6 copy-start.2
  273.2 1.1 copy-start.3
  277.1 1.6 copy-start.2
  280.2 1.1 copy-start.3
  285.9 1.6 copy-start.2
  288.9 1.1 copy-start.3
  298.0 1.6 copy-start.2
  301.0 1.1 copy-start.3
  305.0 1.6 copy-start.2
  308.1 1.1 copy-start.3
  317.1 1.6 copy-start.2
  320.2 1.1 copy-start.3
  422.0 1.1 copy-start.7
  656.2 12.1 %copy-start.5 = (bf16[1,256,3072]{2,1,0:T(8,128)(2,1)S(1)}, bf16[1,256,3072]{2,1,0:T(8,128)(2,1)}, u32[]{:S(2)}) copy-start(bf16[1,256,3072]{2,1,0:T(8,128)(2,1)} %param.13) | copy-start | bytes 4718596
  668.3 4.0 copy-start.1
Sparse Core Ops, SparseCore 0:
  9.7 163.2 all-gather.2
  183.1 71.5 all-gather.4
  422.2 233.9 reduce-scatter.1
where the time goes:
time: 682 us; the launch traced here: 679 us
  waiting for transfers between devices  465 us (68%)
  matrix products  75.4 us (11%)
  local copies, waits for them, and re-layouts  62.5 us (9%)
  other arithmetic  39.1 us (6%)
  loops' own time  22.7 us (3%)
  between operations  13.9 us (2%)
    reduce_scatter x1, waiting for transfers between devices, body(): lax.psum_scatter(block_terms.astype(jnp.bfloat16), 'ctx', scatter_dimensi...  232 us
    all_gather x1, waiting for transfers between devices, body(): panels = lax.all_gather(qkv_weight, 'fsdp', axis=0, tiled=True)  163 us
    all_gather x1, waiting for transfers between devices, body(): pairs_all = lax.all_gather(pairs_local, 'ctx', axis=0, tiled=True)  69.5 us
    dynamic_update_slice x16, local copies, waits for them, and re-layouts, whole_step(): lax.dynamic_update_slice_in_dim(block_terms, block_grads, shard_id * rows...  14.1 us
    dot_general x6, matrix products, compute(): jnp.einsum('tkgd,skd->kgts', grad_heads, values, preferred_element_type=j...  14 us
    reduce_or x16, other arithmetic, forward_step(): jnp.any(allowed)  13.6 us
  transfers between devices with their start and end apart: 3, of which 3 were waited for; matrix products, arithmetic and copies ran while one was open for 1% of the time, Pallas kernels for 0%

commit v1 on v0

v1 whole, which is shorter than its diff:
```python
import math

import jax
import jax.numpy as jnp
from jax import lax
from jax.experimental import pallas as pl
from jax.experimental.pallas import tpu as pltpu
from jax.sharding import PartitionSpec as P

HEADS = 12
KV_HEADS = 4
HEAD_DIM = 128
BLOCK = 128


epsilon = 1e-05
very_low = -1e30


def attention_kernel(mask_ref, q_ref, do_ref, kv_ref, att_ref, dq_ref, dkv_ref, s_ref, list_ref, count_ref):
    scale = 1.0 / math.sqrt(128)
    position = lax.axis_index("ctx")
    dkv_ref[...] = jnp.zeros_like(dkv_ref)
    for r in range(2):
        def note(j, n):
            list_ref[r, n] = j
            return n + mask_ref[position * 2 + r, j]
        count_ref[r] = lax.fori_loop(0, 32, note, 0)

    def unit(u, carry):
        r, h = u // 4, u % 4
        rows = pl.ds(pl.multiple_of(r * 128, 128), 128)
        cols = [pl.ds(pl.multiple_of(h * 384 + i * 128, 128), 128) for i in range(3)]
        kcol = pl.ds(pl.multiple_of(h * 128, 128), 128)
        vcol = pl.ds(pl.multiple_of(512 + h * 128, 128), 128)
        q = jnp.concatenate([q_ref[rows, c] for c in cols], axis=0)
        do = jnp.concatenate([do_ref[rows, c] for c in cols], axis=0)
        n = count_ref[r]
        pairs = (n + 1) // 2

        def ids(p):
            second = jnp.minimum(2 * p + 1, n - 1)
            return list_ref[r, 2 * p], list_ref[r, second], 2 * p + 1 < n

        def load(p, col):
            a, b, _ = ids(p)
            return jnp.concatenate([kv_ref[pl.ds(pl.multiple_of(a * 128, 128), 128), col],
                                    kv_ref[pl.ds(pl.multiple_of(b * 128, 128), 128), col]], axis=0)

        def score(p, m):
            _, _, valid = ids(p)
            s = lax.dot_general(load(p, kcol), q, (((1,), (1,)), ((), ())), preferred_element_type=jnp.float32) * scale
            low = s[128:]
            low = jnp.where(valid, low, -1e30)
            s_ref[p, :128] = s[:128]
            s_ref[p, 128:] = low
            return jnp.maximum(m, jnp.maximum(jnp.max(s[:128], axis=0, keepdims=True), jnp.max(low, axis=0, keepdims=True)))
        m = lax.fori_loop(0, pairs, score, jnp.full((1, 384), -1e30, jnp.float32))

        def weigh(p, carry):
            total, acc = carry
            _, _, valid = ids(p)
            e = jnp.exp(s_ref[p] - m)
            s_ref[p] = e
            total = total + jnp.sum(e, axis=0, keepdims=True)
            acc = acc + lax.dot_general(load(p, vcol), e.astype(jnp.bfloat16), (((0,), (0,)), ((), ())), preferred_element_type=jnp.float32)
            return total, acc
        total, acc = lax.fori_loop(0, pairs, weigh, (jnp.zeros((1, 384), jnp.float32), jnp.zeros((128, 384), jnp.float32)))
        inverse = 1.0 / total
        out_t = acc * inverse
        out = out_t.T
        for i in range(3):
            att_ref[rows, cols[i]] = out[i * 128:(i + 1) * 128].astype(jnp.bfloat16)
        out_half = out_t.astype(jnp.bfloat16).astype(jnp.float32)
        do_t = do.astype(jnp.float32).T
        delta = jnp.sum(out_half * do_t, axis=0, keepdims=True)

        def back(p, dq_t):
            a, b, valid = ids(p)
            k, v = load(p, kcol), load(p, vcol)
            prob = s_ref[p] * inverse
            dprob = lax.dot_general(v, do, (((1,), (1,)), ((), ())), preferred_element_type=jnp.float32)
            ds = (prob * (dprob - delta)).astype(jnp.bfloat16)
            dv = jnp.dot(prob.astype(jnp.bfloat16), do, preferred_element_type=jnp.float32)
            dk = jnp.dot(ds, q, preferred_element_type=jnp.float32) * scale
            dq_t = dq_t + lax.dot_general(k, ds, (((0,), (0,)), ((), ())), preferred_element_type=jnp.float32)

            def put(block, lo):
                where = pl.ds(pl.multiple_of(block * 128, 128), 128)
                dkv_ref[where, kcol] = (dkv_ref[where, kcol].astype(jnp.float32) + dk[lo:lo + 128]).astype(jnp.bfloat16)
                dkv_ref[where, vcol] = (dkv_ref[where, vcol].astype(jnp.float32) + dv[lo:lo + 128]).astype(jnp.bfloat16)
            put(a, 0)
            pl.when(valid)(lambda: put(b, 128))
            return dq_t
        dq = lax.fori_loop(0, pairs, back, jnp.zeros((128, 384), jnp.float32)).T * scale
        for i in range(3):
            dq_ref[rows, cols[i]] = dq[i * 128:(i + 1) * 128].astype(jnp.bfloat16)
        return carry
    lax.fori_loop(0, 8, unit, 0)

def attention(block_mask, q, do, kv):
    vm = pl.BlockSpec(memory_space=pltpu.VMEM)
    return pl.pallas_call(
        attention_kernel,
        out_shape=(jax.ShapeDtypeStruct((256, 1536), jnp.bfloat16), jax.ShapeDtypeStruct((256, 1536), jnp.bfloat16),
                   jax.ShapeDtypeStruct((4096, 1024), jnp.bfloat16)),
        in_specs=[pl.BlockSpec(memory_space=pltpu.SMEM), vm, vm, vm],
        out_specs=(vm, vm, vm),
        scratch_shapes=[pltpu.VMEM((16, 256, 384), jnp.float32), pltpu.SMEM((2, 33), jnp.int32), pltpu.SMEM((2,), jnp.int32)],
        compiler_params=pltpu.CompilerParams(vmem_limit_bytes=60 << 20),
        name="attention",
    )(block_mask, q, do, kv)


def body(tokens, norm_gain, qkv_weight, block_mask, out_grad):
    rows_here = tokens.shape[1]
    group_size = HEADS // KV_HEADS
    query_width = HEADS * HEAD_DIM
    key_width = KV_HEADS * HEAD_DIM
    score_scale = 1.0 / math.sqrt(HEAD_DIM)
    cycle_size = lax.axis_size("ctx")
    position = lax.axis_index("ctx")
    blocks_here = rows_here // BLOCK
    inputs = tokens[0].astype(jnp.float32)
    inv_rms = lax.rsqrt(jnp.mean(inputs * inputs, axis=1, keepdims=True) + epsilon)
    normed = (inputs * inv_rms * norm_gain).astype(jnp.bfloat16)
    panels = lax.all_gather(qkv_weight, "fsdp", axis=0, tiled=True)
    projected = jnp.dot(normed, panels, preferred_element_type=jnp.float32).astype(jnp.bfloat16)
    pairs_all = lax.all_gather(projected[:, query_width:], "ctx", axis=0, tiled=True)
    attended, query_rows_grad, block_terms = attention(block_mask, projected[:, :query_width], out_grad[0], pairs_all)
    pair_grads = lax.psum_scatter(
        block_terms, "ctx", scatter_dimension=0, tiled=True
    ).astype(jnp.float32)
    projected_grad = jnp.concatenate([query_rows_grad, pair_grads.astype(jnp.bfloat16)], axis=1)
    normed_grad = lax.dot_general(
        projected_grad, panels, (((1,), (1,)), ((), ())), preferred_element_type=jnp.float32
    )
    scaled = normed_grad * norm_gain
    token_grad = inv_rms * scaled - inputs * inv_rms**3 * jnp.mean(
        scaled * inputs, axis=1, keepdims=True
    )
    return (attended[None], token_grad.astype(jnp.bfloat16)[None])


def solution(mesh):
    in_specs = (P("fsdp", "ctx", None), P(), P("fsdp", None), P(), P("fsdp", "ctx", None))
    out_specs = (P("fsdp", "ctx", None), P("fsdp", "ctx", None))
    return jax.shard_map(body, mesh=mesh, in_specs=in_specs, out_specs=out_specs, check_vma=False)
```

time: 682 us -> 452 us (0.66)
  waiting for transfers between devices: 465 us -> 378 us
  local copies, waits for them, and re-layouts: 62.5 us -> 1.81 us
  matrix products: 75.4 us -> 19.6 us
  other arithmetic: 39.1 us -> 5.8 us
  Pallas kernels: 0 us -> 33.2 us
  loops' own time: 22.7 us -> 0 us
    reduce_scatter x1, waiting for transfers between devices: 232 us -> 143 us  [body(): lax.psum_scatter(block_terms, 'ctx', scatter_dimension=0, tiled=True)]
    dot_general x42 -> x0, matrix products: 55.2 us -> none  [the longest x6 14 us: compute(): jnp.einsum('tkgd,skd->kgts', grad_heads, values, preferred_element_type=j...]
    pallas_call x0 -> x1, Pallas kernels: none -> 33.2 us  [attention(): pl.pallas_call(attention_kernel, out_shape=(jax.ShapeDtypeStruct((256, 15...]
    reduce_or x32 -> x0, other arithmetic: 25.6 us -> none  [the longest x16 13.6 us: forward_step(): jnp.any(allowed)]
    another operation x34 -> x0, loops' own time: 22.7 us -> none  [the longest x1 11.6 us: body(): lax.fori_loop(0, cycle_size, forward_step, initial)]
    while x68 -> x0, local copies, waits for them, and re-layouts: 16.3 us -> none  [the longest x3 13.6 us: body(): lax.fori_loop(0, cycle_size, forward_step, initial)]
    dynamic_update_slice x16 -> x0, local copies, waits for them, and re-layouts: 14.1 us -> none  [whole_step(): lax.dynamic_update_slice_in_dim(block_terms, block_grads, shard_id * rows...]
    slice x13 -> x1, local copies, waits for them, and re-layouts: 13.8 us -> 0.86 us  [body(): projected[:, query_width:]]
where the time goes in v1:
time: 452 us
  waiting for transfers between devices  378 us (84%)
  Pallas kernels  33.2 us (7%)
  matrix products  19.6 us (4%)
  between operations  13.8 us (3%)
  other arithmetic  5.8 us (1%)
    all_gather x1, waiting for transfers between devices, body(): panels = lax.all_gather(qkv_weight, 'fsdp', axis=0, tiled=True)  163 us
    reduce_scatter x1, waiting for transfers between devices, body(): lax.psum_scatter(block_terms, 'ctx', scatter_dimension=0, tiled=True)  143 us
    all_gather x1, waiting for transfers between devices, body(): lax.all_gather(projected[:, query_width:], 'ctx', axis=0, tiled=True)  70.7 us
    pallas_call x1, Pallas kernels, attention(): pl.pallas_call(attention_kernel, out_shape=(jax.ShapeDtypeStruct((256, 15...  33.2 us
    dot_general x1, matrix products, body(): lax.dot_general(projected_grad, panels, (((1,), (1,)), ((), ())), preferr...  11.6 us
  transfers between devices with their start and end apart: 3, of which 3 were waited for; matrix products, arithmetic and copies ran while one was open for 1% of the time, Pallas kernels for 0%

profile of v1, /device:TPU:0, one launch (start us, length us, event | category | flops | bytes accessed | tf_op | source)
XLA Modules:
  0.0 452.2 jit_solution(12828670923209972135)
XLA Ops:
  7.2 0.0 copy-start
  7.2 0.0 copy-start.2
  7.2 0.0 all-gather.3.cloned.1.call-start
  7.2 0.7 all-gather.3.cloned.1.call-update
  7.9 0.0 all-gather.5.cloned.1.call-start
  8.0 1.8 fusion
  9.8 163.2 %all-gather.3.cloned.1.call-done = bf16[3072,2560]{1,0:T(8,128)(2,1)} async-done(((bf16[384,2560]{1,0:T(8,128)(2,1)}), bf16[3072,2560]{1,0:T(8,128)(2,1)}) %all-gather.3.cloned.1.call-update) | async-done | bytes 15728656 | tf_op jit(solution)/shard_map/all_gather | solution.py:127
  172.9 0.0 copy-done
  172.9 0.0 copy-done.2
  172.9 8.0 %convolution_convert_fusion = bf16[256,2560]{1,0:T(8,128)(2,1)S(1)} fusion(bf16[3072,2560]{1,0:T(8,128)(2,1)} %all-gather.3.cloned.1.call-done, bf16[1,256,3072]{2,1,0:T(8,128)(2,1)S(1)} %copy-done, f32[3072]{0:T(1024)S(1)} %copy-done.2, f32[256]{0:T(256)S(1)} %get-tuple-element.9), kind=kOutput, calls=%fused_computation.5 | convolution fusion | flops 4030332928 | bytes 18625536 | tf_op jit(solution)/shard_map/dot_general | solution.py:128
  180.9 0.9 slice.9
  181.8 0.0 all-gather.5.cloned.1.call-update
  181.8 0.0 reduce-scatter.2.cloned.1.call-start
  181.8 0.9 slice.8.q_ref
  182.8 70.7 %all-gather.5.cloned.1.call-done.kv_ref = bf16[4096,1024]{1,0:T(8,128)(2,1)} async-done(((bf16[256,1024]{1,0:T(8,128)(2,1)}), bf16[4096,1024]{1,0:T(8,128)(2,1)}) %all-gather.5.cloned.1.call-update) | async-done | bytes 8388624 | tf_op jit(solution)/shard_map/all_gather | solution.py:129
  253.5 33.2 %attention.1 = (bf16[256,1536]{1,0:T(8,128)(2,1)}, bf16[256,1536]{1,0:T(8,128)(2,1)}, bf16[4096,1024]{1,0:T(8,128)(2,1)}) custom-call(s32[32,32]{1,0:T(8,128)} %mask_ref.1, bf16[256,1536]{1,0:T(8,128)(2,1)} %slice.8.q_ref, bf16[256,1536]{1,0:T(8,128)(2,1)} %bitcast.15, bf16[4096,1024]{1,0:T(8,128)(2,1)} %all-gather.5.cloned.1.call-done.kv_ref), custom_call_target="tpu_custom_call" | custom-call | tf_op jit(solution)/shard_map/attention/pallas_call | solution.py:103
  286.7 0.0 copy-start.1
  286.7 0.0 reduce-scatter.2.cloned.1.call-update
  286.7 143.4 %reduce-scatter.2.cloned.1.call-done = bf16[256,1024]{1,0:T(8,128)(2,1)} async-done(((bf16[4096,1024]{1,0:T(8,128)(2,1)}), bf16[256,1024]{1,0:T(8,128)(2,1)}) %reduce-scatter.2.cloned.1.call-update) | async-done | bytes 524304 | tf_op jit(solution)/shard_map/reduce_scatter | solution.py:131
  430.1 0.0 copy-done.1
  430.1 11.6 %fusion.6 = (f32[256]{0:T(256)S(1)}, f32[256,3072]{1,0:T(8,128)}) fusion(bf16[1,256,3072]{2,1,0:T(8,128)(2,1)S(1)} %copy-done, f32[3072]{0:T(1024)S(1)} %copy-done.2, bf16[3072,2560]{1,0:T(8,128)(2,1)} %all-gather.3.cloned.1.call-done, bf16[256,1024]{1,0:T(8,128)(2,1)} %reduce-scatter.2.cloned.1.call-done, bf16[256,1536]{1,0:T(8,128)(2,1)S(1)} %copy-done.1), kind=kOutput, calls=%fused_computation.12 | convolution fusion | flops 4032298752 | bytes 21771264 | tf_op jit(solution)/shard_map/dot_general | solution.py:135
  441.7 4.0 fusion.7
  (2 shorter events, 0.0 us)
Async XLA Ops:
  7.2 165.8 %copy-start = (bf16[1,256,3072]{2,1,0:T(8,128)(2,1)S(1)}, bf16[1,256,3072]{2,1,0:T(8,128)(2,1)}, u32[]{:S(2)}) copy-start(bf16[1,256,3072]{2,1,0:T(8,128)(2,1)} %param.5) | copy-start | bytes 4718596
  7.2 165.8 %copy-start.2 = (f32[3072]{0:T(1024)S(1)}, f32[3072]{0:T(1024)}, u32[]{:S(2)}) copy-start(f32[3072]{0:T(1024)} %param.6) | copy-start | bytes 36868
  7.2 165.7 %all-gather.3.cloned.1.call-start = ((), (), s32[]{:S(2)}) async-start(), calls=%async_computation.1 | async-start | bytes 17694720 | tf_op jit(solution)/shard_map/all_gather | solution.py:127
  7.9 245.6 %all-gather.5.cloned.1.call-start = ((), (), s32[]{:S(2)}) async-start(), calls=%async_computation.2 | async-start | bytes 8912896 | tf_op jit(solution)/shard_map/all_gather | solution.py:129
  181.8 248.3 %reduce-scatter.2.cloned.1.call-start = ((), (), s32[]{:S(2)}) async-start(), calls=%async_computation.3 | async-start | bytes 8912896 | tf_op jit(solution)/shard_map/reduce_scatter | solution.py:131
  286.7 143.4 %copy-start.1 = (bf16[256,1536]{1,0:T(8,128)(2,1)S(1)}, bf16[256,1536]{1,0:T(8,128)(2,1)}, u32[]{:S(2)}) copy-start(bf16[256,1536]{1,0:T(8,128)(2,1)} %get-tuple-element.6) | copy-start | bytes 2359300
Sparse Core Ops, SparseCore 0:
  9.7 163.2 all-gather.2
  181.9 71.5 all-gather.4
  286.8 143.2 reduce-scatter.1

commit v2 on v1

--- a/solution.py
+++ b/solution.py
@@ -15,6 +15,244 @@
 
 epsilon = 1e-05
 very_low = -1e30
+
+
+MESH = pl.DeviceIdType.MESH
+D = 3072
+KEYS = pl.ds(1536, 1024)
+QUERIES = pl.ds(0, 1536)
+
+
+class Place:
+    def __init__(self):
+        self.i = lax.axis_index("ctx")
+        self.f = lax.axis_index("fsdp")
+        self.c = self.i % 2
+        self.y = (self.i // 2) % 4
+        self.z = (self.i // 8) * 2 + self.f // 4
+        self.x = self.f % 4
+
+    def ids(self, dx=0, dy=0, dz=0, swap=False):
+        x, y, z = (self.x + dx) % 4, (self.y + dy) % 4, (self.z + dz) % 4
+        c = 1 - self.c if swap else self.c
+        return ((z // 2) * 4 + y) * 2 + c, (z % 2) * 4 + x
+
+
+class Net:
+    def __init__(self, send_sem, recv_sem):
+        self.send_sem, self.recv_sem, self.copies = send_sem, recv_sem, {}
+
+    def send(self, name, src, dst, to):
+        k = len(self.copies)
+        copy = pltpu.make_async_remote_copy(
+            src_ref=src, dst_ref=dst, send_sem=self.send_sem.at[k], recv_sem=self.recv_sem.at[k],
+            device_id=to, device_id_type=MESH)
+        copy.start()
+        self.copies[name] = copy
+
+    def recv(self, name):
+        self.copies[name].wait_recv()
+
+    def drain(self):
+        for copy in self.copies.values():
+            copy.wait_send()
+
+
+def greet(place):
+    barrier = pltpu.get_barrier_semaphore()
+    peers = [place.ids(dx=1), place.ids(dx=-1), place.ids(dy=1), place.ids(dy=-1),
+             place.ids(dz=1), place.ids(dz=-1), place.ids(swap=True)]
+    for peer in peers:
+        pl.semaphore_signal(barrier, inc=1, device_id=peer, device_id_type=MESH)
+    pl.semaphore_wait(barrier, len(peers))
+
+
+def rows_at(start, count):
+    return pl.ds(pl.multiple_of(start, 32), count)
+
+
+class WeightGather:
+    def __init__(self, net, place, tag, shard, whole, cols):
+        self.net, self.p, self.tag, self.shard, self.whole, self.cols = net, place, tag, shard, whole, cols
+
+    def at(self, dx, lo, count):
+        shard_id = (self.p.f // 4) * 4 + (self.p.x + dx) % 4
+        return self.whole.at[rows_at(shard_id * 384 + self.p.c * 192 + lo, count), self.cols]
+
+    def own(self, lo, count):
+        return self.shard.at[rows_at(self.p.c * 192 + lo, count), self.cols]
+
+    def cross(self, dx, lo):
+        shard_id = (1 - self.p.f // 4) * 4 + (self.p.x + dx) % 4
+        return self.whole.at[rows_at(shard_id * 384 + self.p.c * 192 + lo, 96), self.cols]
+
+    def put(self, name, piece, to, src=None):
+        self.net.send(self.tag + name, piece if src is None else src, piece, to)
+
+    def start_x(self):
+        self.put("x+", self.at(0, 0, 192), self.p.ids(dx=1), self.own(0, 192))
+        self.put("x-", self.at(0, 0, 192), self.p.ids(dx=-1), self.own(0, 192))
+
+    def start_z(self):
+        self.put("z+0", self.at(0, 0, 96), self.p.ids(dz=1), self.own(0, 96))
+        self.put("z-0", self.at(0, 96, 96), self.p.ids(dz=-1), self.own(96, 96))
+
+    def got(self, name):
+        self.net.recv(self.tag + name)
+
+    def first(self):
+        self.got("x+")
+        self.put("x+2", self.at(-1, 0, 96), self.p.ids(dx=1))
+        self.got("x-")
+        self.put("x-2", self.at(1, 96, 96), self.p.ids(dx=-1))
+        for dx in (-1, 1):
+            self.put("z+%d" % dx, self.at(dx, 0, 96), self.p.ids(dz=1))
+            self.put("z-%d" % dx, self.at(dx, 96, 96), self.p.ids(dz=-1))
+            self.put("c%d" % dx, self.at(dx, 0, 192), self.p.ids(swap=True))
+
+    def second(self):
+        for sign, lo, dz in (("+", 0, 1), ("-", 96, -1)):
+            self.got("x%s2" % sign)
+            self.put("z%s2" % sign, self.at(2, lo, 96), self.p.ids(dz=dz))
+            self.put("c2%s" % sign, self.at(2, lo, 96), self.p.ids(swap=True))
+
+    def third(self):
+        for dx in (0, -1, 1, 2):
+            for sign, lo in (("+", 0), ("-", 96)):
+                self.got("z%s%d" % (sign, dx))
+                self.put("cz%s%d" % (sign, dx), self.cross(dx, lo), self.p.ids(swap=True))
+
+    def last(self):
+        for name in ("c-1", "c1", "c2+", "c2-"):
+            self.got(name)
+        for dx in (0, -1, 1, 2):
+            for sign in "+-":
+                self.got("cz%s%d" % (sign, dx))
+
+
+def project_kernel(tok_ref, gain_ref, shard, q_ref, kv_all, w_all, w_vm, normed, kv_own, relay, send_sem, recv_sem,
+                   local_sem):
+    p = Place()
+    net = Net(send_sem, recv_sem)
+    greet(p)
+    keys = WeightGather(net, p, "k", shard, w_vm, KEYS)
+    queries = WeightGather(net, p, "q", shard, w_vm, QUERIES)
+    keys.start_x()
+    keys.start_z()
+    mine = pltpu.make_async_copy(shard, w_vm.at[rows_at(p.f * 384, 384)], local_sem.at[0])
+    mine.start()
+
+    @pl.loop(0, 8)
+    def _(t):
+        rows = pl.ds(pl.multiple_of(t * 32, 32), 32)
+        x = tok_ref[rows, :].astype(jnp.float32)
+        inv_rms = lax.rsqrt(jnp.mean(x * x, axis=1, keepdims=True) + epsilon)
+        normed[rows, :] = (x * inv_rms * gain_ref[...]).astype(jnp.bfloat16)
+
+    keys.first()
+    queries.start_x()
+    keys.second()
+    queries.start_z()
+    keys.third()
+    keys.last()
+    mine.wait()
+
+    @pl.loop(0, 4)
+    def _(t):
+        cols = pl.ds(pl.multiple_of(t * 256, 256), 256)
+        part = jnp.dot(normed[...], w_vm[:, pl.ds(pl.multiple_of(1536 + t * 256, 256), 256)],
+                       preferred_element_type=jnp.float32)
+        kv_own[:, cols] = part.astype(jnp.bfloat16)
+
+    keep_keys = pltpu.make_async_copy(w_vm.at[:, KEYS], w_all.at[:, KEYS], local_sem.at[1])
+    keep_keys.start()
+
+    def home(dy=0, dz=0, lo=0, count=256):
+        who, _ = p.ids(dy=dy, dz=dz)
+        return kv_all.at[rows_at(who * 256 + lo, count)]
+
+    def put(name, piece, to, src=None):
+        net.send(name, piece if src is None else src, piece, to)
+
+    swap, up, down, north, south = p.ids(swap=True), p.ids(dz=1), p.ids(dz=-1), p.ids(dy=1), p.ids(dy=-1)
+    put("y+", home(), north, kv_own)
+    put("y-", home(), south, kv_own)
+    put("h+", relay.at[0], up, kv_own.at[:128])
+    put("h-", relay.at[1], down, kv_own.at[128:])
+    put("cy0", home(), swap, kv_own)
+    stay = pltpu.make_async_copy(kv_own, home(), local_sem.at[2])
+    stay.start()
+
+    queries.first()
+    net.recv("h+")
+    put("r+", home(dz=-1, count=128), up, relay.at[0])
+    net.recv("h-")
+    put("r-", home(dz=1, lo=128, count=128), down, relay.at[1])
+    queries.second()
+    for sign, lo in (("+", 0), ("-", 128)):
+        net.recv("r" + sign)
+        piece = home(dz=2, lo=lo, count=128)
+        put("ty+" + sign, piece, north)
+        put("ty-" + sign, piece, south)
+        put("ct" + sign, piece, swap)
+    net.recv("y+")
+    put("y+2", home(dy=-1, count=128), north)
+    put("cy-", home(dy=-1), swap)
+    net.recv("y-")
+    put("y-2", home(dy=1, lo=128, count=128), south)
+    put("cy+", home(dy=1), swap)
+    queries.third()
+    queries.last()
+
+    keep_queries = pltpu.make_async_copy(w_vm.at[:, QUERIES], w_all.at[:, QUERIES], local_sem.at[3])
+    keep_queries.start()
+
+    net.recv("ty++")
+    put("ty+2", home(dy=-1, dz=2, count=128), north)
+    put("ct-a", home(dy=-1, dz=2, count=128), swap)
+    net.recv("ty--")
+    put("ty-2", home(dy=1, dz=2, lo=128, count=128), south)
+    put("ct+b", home(dy=1, dz=2, lo=128, count=128), swap)
+    net.recv("ty+-")
+    put("ct-b", home(dy=-1, dz=2, lo=128, count=128), swap)
+    net.recv("ty-+")
+    put("ct+a", home(dy=1, dz=2, count=128), swap)
+
+    @pl.loop(0, 6)
+    def _(t):
+        cols = pl.ds(pl.multiple_of(t * 256, 256), 256)
+        q_ref[:, cols] = jnp.dot(normed[...], w_vm[:, cols], preferred_element_type=jnp.float32).astype(jnp.bfloat16)
+
+    net.recv("y+2")
+    put("cy2a", home(dy=2, count=128), swap)
+    net.recv("y-2")
+    put("cy2b", home(dy=2, lo=128, count=128), swap)
+    net.recv("ty+2")
+    put("ct2a", home(dy=2, dz=2, count=128), swap)
+    net.recv("ty-2")
+    put("ct2b", home(dy=2, dz=2, lo=128, count=128), swap)
+    for name in ("cy0", "cy-", "cy+", "cy2a", "cy2b", "ct+", "ct-", "ct-a", "ct+b", "ct-b", "ct+a", "ct2a", "ct2b"):
+        net.recv(name)
+    net.drain()
+    for copy in (stay, keep_keys, keep_queries):
+        copy.wait()
+
+
+def project(tokens, gain, shard):
+    vm, anywhere = pl.BlockSpec(memory_space=pltpu.VMEM), pl.BlockSpec(memory_space=pl.ANY)
+    half = jnp.bfloat16
+    return pl.pallas_call(
+        project_kernel,
+        out_shape=(jax.ShapeDtypeStruct((256, 1536), half), jax.ShapeDtypeStruct((4096, 1024), half),
+                   jax.ShapeDtypeStruct((3072, 2560), half)),
+        in_specs=[vm, vm, anywhere],
+        out_specs=(vm, anywhere, anywhere),
+        scratch_shapes=[pltpu.VMEM((3072, 2560), half), pltpu.VMEM((256, 3072), half), pltpu.VMEM((256, 1024), half),
+                        pltpu.VMEM((2, 128, 1024), half), pltpu.SemaphoreType.DMA((80,)),
+                        pltpu.SemaphoreType.DMA((80,)), pltpu.SemaphoreType.DMA((4,))],
+        compiler_params=pltpu.CompilerParams(vmem_limit_bytes=60 << 20, collective_id=0, has_side_effects=True),
+        name="project",
+    )(tokens, gain, shard)
 
 
 def attention_kernel(mask_ref, q_ref, do_ref, kv_ref, att_ref, dq_ref, dkv_ref, s_ref, list_ref, count_ref):
@@ -123,11 +361,8 @@
     blocks_here = rows_here // BLOCK
     inputs = tokens[0].astype(jnp.float32)
     inv_rms = lax.rsqrt(jnp.mean(inputs * inputs, axis=1, keepdims=True) + epsilon)
-    normed = (inputs * inv_rms * norm_gain).astype(jnp.bfloat16)
-    panels = lax.all_gather(qkv_weight, "fsdp", axis=0, tiled=True)
-    projected = jnp.dot(normed, panels, preferred_element_type=jnp.float32).astype(jnp.bfloat16)
-    pairs_all = lax.all_gather(projected[:, query_width:], "ctx", axis=0, tiled=True)
-    attended, query_rows_grad, block_terms = attention(block_mask, projected[:, :query_width], out_grad[0], pairs_all)
+    queries, pairs_all, panels = project(tokens[0], norm_gain[None], qkv_weight)
+    attended, query_rows_grad, block_terms = attention(block_mask, queries, out_grad[0], pairs_all)
     pair_grads = lax.psum_scatter(
         block_terms, "ctx", scatter_dimension=0, tiled=True
     ).astype(jnp.float32)

time: 452 us -> 301 us (0.67)
  waiting for transfers between devices: 378 us -> 145 us
  Pallas kernels: 33.2 us -> 127 us
  matrix products: 19.6 us -> 11.7 us
    all_gather x2 -> x0, waiting for transfers between devices: 234 us -> none  [the longest x1 163 us: body(): panels = lax.all_gather(qkv_weight, 'fsdp', axis=0, tiled=True)]
    pallas_call x0 -> x1, Pallas kernels: none -> 93.5 us  [project(): pl.pallas_call(project_kernel, out_shape=(jax.ShapeDtypeStruct((256, 1536...]
    dot_general x1 -> x0, matrix products: 7.96 us -> none  [body(): jnp.dot(normed, panels, preferred_element_type=jnp.float32)]
  transfers between devices with their start and end apart: 3 -> 1, of which waited for: 3 -> 1; matrix products, arithmetic and copies ran while one was open for 1% -> 0% of each run, Pallas kernels for 0% -> 0%
where the time goes in v2:
time: 301 us
  waiting for transfers between devices  145 us (48%)
  Pallas kernels  127 us (42%)
  between operations  14 us (5%)
  matrix products  11.7 us (4%)
  other arithmetic  4 us (1%)
    reduce_scatter x1, waiting for transfers between devices, body(): lax.psum_scatter(block_terms, 'ctx', scatter_dimension=0, tiled=True)  145 us
    pallas_call x1, Pallas kernels, project(): pl.pallas_call(project_kernel, out_shape=(jax.ShapeDtypeStruct((256, 1536...  93.5 us
    pallas_call x1, Pallas kernels, attention(): pl.pallas_call(attention_kernel, out_shape=(jax.ShapeDtypeStruct((256, 15...  33.2 us
    dot_general x1, matrix products, body(): lax.dot_general(projected_grad, panels, (((1,), (1,)), ((), ())), preferr...  11.7 us
  transfers between devices with their start and end apart: 1, of which 1 were waited for; matrix products, arithmetic and copies ran while one was open for 0% of the time, Pallas kernels for 0%

profile of v2, /device:TPU:0, one launch (start us, length us, event | category | flops | bytes accessed | tf_op | source)
XLA Modules:
  0.0 301.2 jit_solution(8303871195329602206)
XLA Ops:
  7.2 0.0 reduce-scatter.2.cloned.1.call-start
  7.2 93.5 %project.1 = (bf16[256,1536]{1,0:T(8,128)(2,1)}, bf16[4096,1024]{1,0:T(8,128)(2,1)}, bf16[3072,2560]{1,0:T(8,128)(2,1)}) custom-call(bf16[256,3072]{1,0:T(8,128)(2,1)} %bitcast.10, f32[1,3072]{1,0:T(1,128)} %bitcast.12, bf16[384,2560]{1,0:T(8,128)(2,1)} %shard.1), custom_call_target="tpu_custom_call" | custom-call | tf_op jit(solution)/shard_map/project/pallas_call | solution.py:244
  100.7 33.2 %attention.1 = (bf16[256,1536]{1,0:T(8,128)(2,1)}, bf16[256,1536]{1,0:T(8,128)(2,1)}, bf16[4096,1024]{1,0:T(8,128)(2,1)}) custom-call(s32[32,32]{1,0:T(8,128)} %mask_ref.1, bf16[256,1536]{1,0:T(8,128)(2,1)} %get-tuple-element.8.q_ref, bf16[256,1536]{1,0:T(8,128)(2,1)} %bitcast.11, bf16[4096,1024]{1,0:T(8,128)(2,1)} %get-tuple-element.9.kv_ref), custom_call_target="tpu_custom_call" | custom-call | tf_op jit(solution)/shard_map/attention/pallas_call | solution.py:341
  133.9 0.0 copy-start
  133.9 0.0 copy-start.1
  133.9 0.0 copy-start.2
  133.9 0.0 reduce-scatter.2.cloned.1.call-update
  133.9 144.8 %reduce-scatter.2.cloned.1.call-done = bf16[256,1024]{1,0:T(8,128)(2,1)} async-done(((bf16[4096,1024]{1,0:T(8,128)(2,1)}), bf16[256,1024]{1,0:T(8,128)(2,1)}) %reduce-scatter.2.cloned.1.call-update) | async-done | bytes 524304 | tf_op jit(solution)/shard_map/reduce_scatter | solution.py:366
  278.7 0.0 copy-done
  278.7 0.0 copy-done.1
  278.7 0.0 copy-done.2
  278.7 11.7 %fusion = (f32[256]{0:T(256)S(1)}, f32[256]{0:T(256)S(1)}, f32[256,3072]{1,0:T(8,128)}) fusion(bf16[1,256,3072]{2,1,0:T(8,128)(2,1)S(1)} %copy-done, f32[3072]{0:T(1024)S(1)} %copy-done.1, bf16[3072,2560]{1,0:T(8,128)(2,1)} %get-tuple-element.13, bf16[256,1024]{1,0:T(8,128)(2,1)} %reduce-scatter.2.cloned.1.call-done, bf16[256,1536]{1,0:T(8,128)(2,1)S(1)} %copy-done.2), kind=kOutput, calls=%fused_computation.4 | convolution fusion | flops 4033871360 | bytes 21772288 | tf_op jit(solution)/shard_map/dot_general | solution.py:370
  290.4 4.0 %fusion.5 = bf16[1,256,3072]{2,1,0:T(8,128)(2,1)} fusion(f32[256,3072]{1,0:T(8,128)} %get-tuple-element.18, f32[256]{0:T(256)S(1)} %get-tuple-element.19, f32[256]{0:T(256)S(1)} %get-tuple-element.17, f32[256]{0:T(256)S(1)} %get-tuple-element.16, bf16[1,256,3072]{2,1,0:T(8,128)(2,1)S(1)} %copy-done), kind=kLoop, calls=%fused_computation.9 | loop fusion | flops 4718592 | bytes 6294528 | tf_op jit(solution)/shard_map/broadcast_in_dim | solution.py:377
  (1 shorter events, 0.0 us)
Async XLA Ops:
  7.2 271.5 %reduce-scatter.2.cloned.1.call-start = ((), (), s32[]{:S(2)}) async-start(), calls=%async_computation.1 | async-start | bytes 8912896 | tf_op jit(solution)/shard_map/reduce_scatter | solution.py:366
  133.9 144.8 %copy-start = (bf16[1,256,3072]{2,1,0:T(8,128)(2,1)S(1)}, bf16[1,256,3072]{2,1,0:T(8,128)(2,1)}, u32[]{:S(2)}) copy-start(bf16[1,256,3072]{2,1,0:T(8,128)(2,1)} %param.5) | copy-start | bytes 4718596
  133.9 144.8 %copy-start.1 = (f32[3072]{0:T(1024)S(1)}, f32[3072]{0:T(1024)}, u32[]{:S(2)}) copy-start(f32[3072]{0:T(1024)} %param.6) | copy-start | bytes 36868
  133.9 144.8 %copy-start.2 = (bf16[256,1536]{1,0:T(8,128)(2,1)S(1)}, bf16[256,1536]{1,0:T(8,128)(2,1)}, u32[]{:S(2)}) copy-start(bf16[256,1536]{1,0:T(8,128)(2,1)} %get-tuple-element.11) | copy-start | bytes 2359300
Sparse Core Ops, SparseCore 0:
  134.1 144.5 reduce-scatter.1

commit v3 on v2

--- a/solution.py
+++ b/solution.py
@@ -350,31 +350,126 @@
     )(block_mask, q, do, kv)
 
 
+def grads_kernel(tok_ref, gain_ref, dq_ref, terms, w_all, out_ref, w_vm, mine, part, ahead, behind, after, before,
+                 relay, crossed, total, send_sem, recv_sem, local_sem):
+    p = Place()
+    net = Net(send_sem, recv_sem)
+    greet(p)
+    order = [(dz, dy) for dz in (2, 0) for dy in (2, 1, 3, 0)]
+    swap, up, down, north, south = p.ids(swap=True), p.ids(dz=1), p.ids(dz=-1), p.ids(dy=1), p.ids(dy=-1)
+    loads = {}
+    for slot, (dz, dy) in enumerate(order):
+        who, _ = p.ids(dy=dy, dz=dz)
+        other, _ = p.ids(dy=dy, dz=dz, swap=True)
+        net.send("c%d" % slot, terms.at[rows_at(other * 256, 256)], part.at[slot], swap)
+        loads[slot] = pltpu.make_async_copy(terms.at[rows_at(who * 256, 256)], mine.at[slot], local_sem.at[slot])
+        loads[slot].start()
+    weight = pltpu.make_async_copy(w_all, w_vm, local_sem.at[8])
+    weight.start()
+
+    def add(dst, *srcs):
+        @pl.loop(0, dst.shape[0] // 64)
+        def _(t):
+            rows = pl.ds(pl.multiple_of(t * 64, 64), 64)
+            value = dst[rows, :]
+            for src in srcs:
+                value = value + src[rows, :]
+            dst[rows, :] = value
+
+    def pair(slot):
+        loads[slot].wait()
+        net.recv("c%d" % slot)
+        add(mine.at[slot], part.at[slot])
+
+    def far(base, plane):
+        pair(base)
+        net.send("a%d" % plane, mine.at[base, :128], ahead.at[plane], north)
+        net.send("b%d" % plane, mine.at[base, 128:], behind.at[plane], south)
+        pair(base + 1)
+        pair(base + 2)
+
+    def near(base, plane):
+        net.recv("a%d" % plane)
+        add(mine.at[base + 1, :128], ahead.at[plane])
+        net.send("f%d" % plane, mine.at[base + 1], after.at[plane], north)
+        net.recv("b%d" % plane)
+        add(mine.at[base + 2, 128:], behind.at[plane])
+        net.send("g%d" % plane, mine.at[base + 2], before.at[plane], south)
+        pair(base + 3)
+
+    def gathered(base, plane):
+        net.recv("f%d" % plane)
+        net.recv("g%d" % plane)
+        add(mine.at[base + 3], after.at[plane], before.at[plane])
+
+    def query_part(first, last):
+        @pl.loop(first, last)
+        def _(t):
+            cols = pl.ds(pl.multiple_of(t * 256, 256), 256)
+            total[:, cols] = lax.dot_general(dq_ref[...], w_vm[cols, :1536], (((1,), (1,)), ((), ())),
+                                             preferred_element_type=jnp.float32)
+
+    far(0, 0)
+    far(4, 1)
+    near(0, 0)
+    near(4, 1)
+    weight.wait()
+    query_part(0, 12)
+    gathered(0, 0)
+    net.send("h+", mine.at[3, :128], relay.at[0], up)
+    net.send("h-", mine.at[3, 128:], relay.at[1], down)
+    net.recv("h+")
+    net.send("r+", relay.at[0], crossed.at[:128], up)
+    net.recv("h-")
+    net.send("r-", relay.at[1], crossed.at[128:], down)
+    gathered(4, 1)
+    net.recv("r+")
+    net.recv("r-")
+    add(mine.at[7], crossed)
+
+    @pl.loop(0, 12)
+    def _(t):
+        cols = pl.ds(pl.multiple_of(t * 256, 256), 256)
+        total[:, cols] += lax.dot_general(mine[7], w_vm[cols, 1536:], (((1,), (1,)), ((), ())),
+                                          preferred_element_type=jnp.float32)
+
+    @pl.loop(0, 8)
+    def _(t):
+        rows = pl.ds(pl.multiple_of(t * 32, 32), 32)
+        x = tok_ref[rows, :].astype(jnp.float32)
+        inv_rms = lax.rsqrt(jnp.mean(x * x, axis=1, keepdims=True) + epsilon)
+        scaled = total[rows, :] * gain_ref[...]
+        shift = inv_rms * inv_rms * inv_rms * jnp.mean(scaled * x, axis=1, keepdims=True)
+        out_ref[rows, :] = (inv_rms * scaled - x * shift).astype(jnp.bfloat16)
+    net.drain()
+
+
+def input_grads(tokens, gain, dq, terms, weight):
+    vm, anywhere = pl.BlockSpec(memory_space=pltpu.VMEM), pl.BlockSpec(memory_space=pl.ANY)
+    half = jnp.bfloat16
+    return pl.pallas_call(
+        grads_kernel,
+        out_shape=jax.ShapeDtypeStruct((256, 3072), half),
+        in_specs=[vm, vm, vm, anywhere, anywhere],
+        out_specs=vm,
+        scratch_shapes=[pltpu.VMEM((3072, 2560), half), pltpu.VMEM((8, 256, 1024), half),
+                        pltpu.VMEM((8, 256, 1024), half), pltpu.VMEM((2, 128, 1024), half),
+                        pltpu.VMEM((2, 128, 1024), half), pltpu.VMEM((2, 256, 1024), half),
+                        pltpu.VMEM((2, 256, 1024), half), pltpu.VMEM((2, 128, 1024), half),
+                        pltpu.VMEM((256, 1024), half), pltpu.VMEM((256, 3072), jnp.float32),
+                        pltpu.SemaphoreType.DMA((24,)), pltpu.SemaphoreType.DMA((24,)),
+                        pltpu.SemaphoreType.DMA((9,))],
+        compiler_params=pltpu.CompilerParams(vmem_limit_bytes=60 << 20, collective_id=1, has_side_effects=True),
+        name="input_grads",
+    )(tokens, gain, dq, terms, weight)
+
+
 def body(tokens, norm_gain, qkv_weight, block_mask, out_grad):
-    rows_here = tokens.shape[1]
-    group_size = HEADS // KV_HEADS
-    query_width = HEADS * HEAD_DIM
-    key_width = KV_HEADS * HEAD_DIM
-    score_scale = 1.0 / math.sqrt(HEAD_DIM)
-    cycle_size = lax.axis_size("ctx")
-    position = lax.axis_index("ctx")
-    blocks_here = rows_here // BLOCK
-    inputs = tokens[0].astype(jnp.float32)
-    inv_rms = lax.rsqrt(jnp.mean(inputs * inputs, axis=1, keepdims=True) + epsilon)
-    queries, pairs_all, panels = project(tokens[0], norm_gain[None], qkv_weight)
-    attended, query_rows_grad, block_terms = attention(block_mask, queries, out_grad[0], pairs_all)
-    pair_grads = lax.psum_scatter(
-        block_terms, "ctx", scatter_dimension=0, tiled=True
-    ).astype(jnp.float32)
-    projected_grad = jnp.concatenate([query_rows_grad, pair_grads.astype(jnp.bfloat16)], axis=1)
-    normed_grad = lax.dot_general(
-        projected_grad, panels, (((1,), (1,)), ((), ())), preferred_element_type=jnp.float32
-    )
-    scaled = normed_grad * norm_gain
-    token_grad = inv_rms * scaled - inputs * inv_rms**3 * jnp.mean(
-        scaled * inputs, axis=1, keepdims=True
-    )
-    return (attended[None], token_grad.astype(jnp.bfloat16)[None])
+    gain = norm_gain[None]
+    queries, pairs_all, panels = project(tokens[0], gain, qkv_weight)
+    attended, query_grad, block_terms = attention(block_mask, queries, out_grad[0], pairs_all)
+    token_grad = input_grads(tokens[0], gain, query_grad, block_terms, panels)
+    return (attended[None], token_grad[None])
 
 
 def solution(mesh):

time: 301 us -> 229 us (0.76)
  waiting for transfers between devices: 145 us -> 0 us
  Pallas kernels: 127 us -> 225 us
  between operations: 14 us -> 0.65 us
  matrix products: 11.7 us -> 0 us
  other arithmetic: 4 us -> 0 us
    reduce_scatter x1 -> x0, waiting for transfers between devices: 145 us -> none  [body(): lax.psum_scatter(block_terms, 'ctx', scatter_dimension=0, tiled=True)]
    pallas_call x0 -> x1, Pallas kernels: none -> 102 us  [input_grads(): pl.pallas_call(grads_kernel, out_shape=jax.ShapeDtypeStruct((256, 3072),...]
    dot_general x1 -> x0, matrix products: 11.7 us -> none  [body(): lax.dot_general(projected_grad, panels, (((1,), (1,)), ((), ())), preferr...]
    broadcast_in_dim x1 -> x0, other arithmetic: 3.99 us -> none  [body(): return (attended[None], token_grad.astype(jnp.bfloat16)[None])]
    pallas_call x1, Pallas kernels: 33.2 us -> 29.6 us  [attention(): pl.pallas_call(attention_kernel, out_shape=(jax.ShapeDtypeStruct((256, 15...]
  transfers between devices with their start and end apart: 1 -> 0, of which waited for: 1 -> 0; matrix products, arithmetic and copies ran while one was open for 0% -> 0% of each run, Pallas kernels for 0% -> 0%
where the time goes in v3:
time: 229 us
  Pallas kernels  225 us (98%)
  local copies, waits for them, and re-layouts  2.65 us (1%)
    pallas_call x1, Pallas kernels, input_grads(): pl.pallas_call(grads_kernel, out_shape=jax.ShapeDtypeStruct((256, 3072),...  102 us
    pallas_call x1, Pallas kernels, project(): pl.pallas_call(project_kernel, out_shape=(jax.ShapeDtypeStruct((256, 1536...  93.5 us
    pallas_call x1, Pallas kernels, attention(): pl.pallas_call(attention_kernel, out_shape=(jax.ShapeDtypeStruct((256, 15...  29.6 us

profile of v3, /device:TPU:0, one launch (start us, length us, event | category | flops | bytes accessed | tf_op | source)
XLA Modules:
  0.0 228.6 jit_solution(4051288060086133060)
XLA Ops:
  0.6 93.5 %project.1 = (bf16[256,1536]{1,0:T(8,128)(2,1)}, bf16[4096,1024]{1,0:T(8,128)(2,1)}, bf16[3072,2560]{1,0:T(8,128)(2,1)}) custom-call(bf16[256,3072]{1,0:T(8,128)(2,1)} %bitcast.5, f32[1,3072]{1,0:T(1,128)} %bitcast.9, bf16[384,2560]{1,0:T(8,128)(2,1)} %shard.1), custom_call_target="tpu_custom_call" | custom-call | tf_op jit(solution)/shard_map/project/pallas_call | solution.py:244
  94.1 29.6 %attention.1 = (bf16[256,1536]{1,0:T(8,128)(2,1)}, bf16[256,1536]{1,0:T(8,128)(2,1)}, bf16[4096,1024]{1,0:T(8,128)(2,1)}) custom-call(s32[32,32]{1,0:T(8,128)} %mask_ref.1, bf16[256,1536]{1,0:T(8,128)(2,1)} %get-tuple-element.8.q_ref, bf16[256,1536]{1,0:T(8,128)(2,1)} %bitcast.8, bf16[4096,1024]{1,0:T(8,128)(2,1)} %get-tuple-element.9.kv_ref), custom_call_target="tpu_custom_call" | custom-call | tf_op jit(solution)/shard_map/attention/pallas_call | solution.py:341
  123.7 102.1 %input_grads.1 = bf16[256,3072]{1,0:T(8,128)(2,1)} custom-call(bf16[256,3072]{1,0:T(8,128)(2,1)} %bitcast.6, f32[1,3072]{1,0:T(1,128)} %bitcast.10, bf16[256,1536]{1,0:T(8,128)(2,1)} %get-tuple-element.11.dq_ref, bf16[4096,1024]{1,0:T(8,128)(2,1)} %get-tuple-element.12.terms, bf16[3072,2560]{1,0:T(8,128)(2,1)} %get-tuple-element.13.w_all), custom_call_target="tpu_custom_call" | custom-call | tf_op jit(solution)/shard_map/input_grads/pallas_call | solution.py:450
  225.9 2.7 %copy.8 = bf16[1,256,3072]{2,1,0:T(8,128)(2,1)} copy(bf16[1,256,3072]{2,1,0:T(8,128)(2,1)} %bitcast.7) | data formatting | bytes 3145728

commit v4 on v3

--- a/solution.py
+++ b/solution.py
@@ -37,6 +37,9 @@
         c = 1 - self.c if swap else self.c
         return ((z // 2) * 4 + y) * 2 + c, (z % 2) * 4 + x
 
+    def mate(self, d):
+        return (self.i + d) % 16, self.f
+
 
 class Net:
     def __init__(self, send_sem, recv_sem):
@@ -60,11 +63,25 @@
 
 def greet(place):
     barrier = pltpu.get_barrier_semaphore()
-    peers = [place.ids(dx=1), place.ids(dx=-1), place.ids(dy=1), place.ids(dy=-1),
-             place.ids(dz=1), place.ids(dz=-1), place.ids(swap=True)]
+    peers = [place.ids(dx=1), place.ids(dx=-1), place.ids(dz=1), place.ids(dz=-1)]
+    peers += [place.mate(d) for d in range(1, 16)]
     for peer in peers:
         pl.semaphore_signal(barrier, inc=1, device_id=peer, device_id_type=MESH)
     pl.semaphore_wait(barrier, len(peers))
+
+
+def chosen(mask_ref, place, r):
+    ones = jnp.sum(mask_ref[pl.ds(place.i * 2 + r, 1), :].astype(jnp.float32), axis=1, keepdims=True)
+    return jnp.where(ones > 31.5, 1.0, 0.0)
+
+
+def cut(rows, mask_ref, place, pieces):
+    flags = [chosen(mask_ref, place, r) for r in range(2)]
+    for j in range(16):
+        cols = slice((j // 4) * 384, (j // 4 + 1) * 384)
+        part = [rows[r * 128 + (j % 4) * 32:r * 128 + (j % 4 + 1) * 32, cols].astype(jnp.float32) * flags[r]
+                for r in range(2)]
+        pieces[j] = (part[0] + part[1]).astype(jnp.bfloat16)
 
 
 def rows_at(start, count):
@@ -130,8 +147,8 @@
                 self.got("cz%s%d" % (sign, dx))
 
 
-def project_kernel(tok_ref, gain_ref, shard, q_ref, kv_all, w_all, w_vm, normed, kv_own, relay, send_sem, recv_sem,
-                   local_sem):
+def project_kernel(tok_ref, gain_ref, mask_ref, do_ref, shard, q_ref, kv_all, w_all, wide_ref, w_vm, normed, kv_own,
+                   relay, q_cut, do_cut, q_box, do_box, send_sem, recv_sem, local_sem):
     p = Place()
     net = Net(send_sem, recv_sem)
     greet(p)
@@ -149,6 +166,7 @@
         inv_rms = lax.rsqrt(jnp.mean(x * x, axis=1, keepdims=True) + epsilon)
         normed[rows, :] = (x * inv_rms * gain_ref[...]).astype(jnp.bfloat16)
 
+    cut(do_ref, mask_ref, p, do_cut)
     keys.first()
     queries.start_x()
     keys.second()
@@ -202,6 +220,8 @@
     put("y-2", home(dy=1, lo=128, count=128), south)
     put("cy+", home(dy=1), swap)
     queries.third()
+    for d in range(1, 16):
+        put("do%d" % d, do_box.at[d - 1], p.mate(d), do_cut.at[(p.i + d) % 16])
     queries.last()
 
     keep_queries = pltpu.make_async_copy(w_vm.at[:, QUERIES], w_all.at[:, QUERIES], local_sem.at[3])
@@ -223,6 +243,10 @@
         cols = pl.ds(pl.multiple_of(t * 256, 256), 256)
         q_ref[:, cols] = jnp.dot(normed[...], w_vm[:, cols], preferred_element_type=jnp.float32).astype(jnp.bfloat16)
 
+    cut(q_ref, mask_ref, p, q_cut)
+    for d in range(1, 16):
+        put("qq%d" % d, q_box.at[d - 1], p.mate(d), q_cut.at[(p.i + d) % 16])
+
     net.recv("y+2")
     put("cy2a", home(dy=2, count=128), swap)
     net.recv("y-2")
@@ -233,131 +257,196 @@
     put("ct2b", home(dy=2, dz=2, lo=128, count=128), swap)
     for name in ("cy0", "cy-", "cy+", "cy2a", "cy2b", "ct+", "ct-", "ct-a", "ct+b", "ct-b", "ct+a", "ct2a", "ct2b"):
         net.recv(name)
+    for name, box, own, cols in (("qq", q_box, q_cut, slice(0, 384)), ("do", do_box, do_cut, slice(384, 768))):
+        value = own[p.i]
+        for d in range(1, 16):
+            net.recv("%s%d" % (name, d))
+            value = value + box[d - 1]
+        wide_ref[:, cols] = value
     net.drain()
     for copy in (stay, keep_keys, keep_queries):
         copy.wait()
 
 
-def project(tokens, gain, shard):
+def project(tokens, gain, mask, out_grad, shard):
     vm, anywhere = pl.BlockSpec(memory_space=pltpu.VMEM), pl.BlockSpec(memory_space=pl.ANY)
     half = jnp.bfloat16
     return pl.pallas_call(
         project_kernel,
         out_shape=(jax.ShapeDtypeStruct((256, 1536), half), jax.ShapeDtypeStruct((4096, 1024), half),
-                   jax.ShapeDtypeStruct((3072, 2560), half)),
-        in_specs=[vm, vm, anywhere],
-        out_specs=(vm, anywhere, anywhere),
+                   jax.ShapeDtypeStruct((3072, 2560), half), jax.ShapeDtypeStruct((32, 768), half)),
+        in_specs=[vm, vm, vm, vm, anywhere],
+        out_specs=(vm, anywhere, anywhere, vm),
         scratch_shapes=[pltpu.VMEM((3072, 2560), half), pltpu.VMEM((256, 3072), half), pltpu.VMEM((256, 1024), half),
-                        pltpu.VMEM((2, 128, 1024), half), pltpu.SemaphoreType.DMA((80,)),
-                        pltpu.SemaphoreType.DMA((80,)), pltpu.SemaphoreType.DMA((4,))],
+                        pltpu.VMEM((2, 128, 1024), half), pltpu.VMEM((16, 32, 384), half),
+                        pltpu.VMEM((16, 32, 384), half), pltpu.VMEM((15, 32, 384), half),
+                        pltpu.VMEM((15, 32, 384), half), pltpu.SemaphoreType.DMA((120,)),
+                        pltpu.SemaphoreType.DMA((120,)), pltpu.SemaphoreType.DMA((4,))],
         compiler_params=pltpu.CompilerParams(vmem_limit_bytes=60 << 20, collective_id=0, has_side_effects=True),
         name="project",
-    )(tokens, gain, shard)
-
-
-def attention_kernel(mask_ref, q_ref, do_ref, kv_ref, att_ref, dq_ref, dkv_ref, s_ref, list_ref, count_ref):
-    scale = 1.0 / math.sqrt(128)
+    )(tokens, gain, mask, out_grad, shard)
+
+
+WIDEST = 6
+FACTOR = math.log2(math.e) / math.sqrt(128)
+SCALE = 1.0 / math.sqrt(128)
+CHUNK = 1024
+
+
+def dot_nt(a, b):
+    return lax.dot_general(a, b, (((1,), (1,)), ((), ())), preferred_element_type=jnp.float32)
+
+
+def dot_tn(a, b):
+    return lax.dot_general(a, b, (((0,), (0,)), ((), ())), preferred_element_type=jnp.float32)
+
+
+def dot_nn(a, b):
+    return jnp.dot(a, b, preferred_element_type=jnp.float32)
+
+
+def wide_row(wide_ref, kv_ref, att_ref, dkv_ref, s_ref, head):
+    kcol = pl.ds(pl.multiple_of(head * 128, 128), 128)
+    vcol = pl.ds(pl.multiple_of(512 + head * 128, 128), 128)
+    blank = jnp.zeros((32, 128), jnp.bfloat16)
+    q = jnp.concatenate([wide_ref[:, i * 128:(i + 1) * 128] for i in range(3)] + [blank], axis=0)
+    do = jnp.concatenate([wide_ref[:, 384 + i * 128:384 + (i + 1) * 128] for i in range(3)] + [blank], axis=0)
+    steps = 4096 // CHUNK
+
+    def at(c):
+        return pl.ds(pl.multiple_of(c * CHUNK, CHUNK), CHUNK)
+
+    def score(c, m):
+        s = dot_nt(kv_ref[at(c), kcol], q) * FACTOR
+        s_ref[at(c), :] = s
+        return jnp.maximum(m, jnp.max(s, axis=0, keepdims=True))
+    m = lax.fori_loop(0, steps, score, jnp.full((1, 128), -1e30, jnp.float32))
+
+    def weigh(c, carry):
+        total, acc = carry
+        e = jnp.exp2(s_ref[at(c), :] - m)
+        s_ref[at(c), :] = e
+        total = total + jnp.sum(e, axis=0, keepdims=True)
+        return total, acc + dot_tn(kv_ref[at(c), vcol], e.astype(jnp.bfloat16))
+    total, acc = lax.fori_loop(0, steps, weigh,
+                               (jnp.zeros((1, 128), jnp.float32), jnp.zeros((128, 128), jnp.float32)))
+    inverse = 1.0 / total
+    out_t = acc * inverse
+    out = out_t.T.astype(jnp.bfloat16)
+    for i in range(3):
+        att_ref[:, i * 128:(i + 1) * 128] = out[i * 32:(i + 1) * 32]
+    delta = jnp.sum(out_t.astype(jnp.bfloat16).astype(jnp.float32) * do.astype(jnp.float32).T, axis=0, keepdims=True)
+    share = jnp.broadcast_to(inverse, (128, 128)).T
+    do_share = (do.astype(jnp.float32) * share).astype(jnp.bfloat16)
+    q_share = (q.astype(jnp.float32) * (share * SCALE)).astype(jnp.bfloat16)
+
+    def back(c, dq_t):
+        e = s_ref[at(c), :]
+        ds = (e * (dot_nt(kv_ref[at(c), vcol], do) - delta)).astype(jnp.bfloat16)
+        dkv_ref[at(c), vcol] = dot_nn(e.astype(jnp.bfloat16), do_share).astype(jnp.bfloat16)
+        dkv_ref[at(c), kcol] = dot_nn(ds, q_share).astype(jnp.bfloat16)
+        return dq_t + dot_tn(kv_ref[at(c), kcol], ds)
+    dq_t = lax.fori_loop(0, steps, back, jnp.zeros((128, 128), jnp.float32))
+    dq = (dq_t * (inverse * SCALE)).T.astype(jnp.bfloat16)
+    for i in range(3):
+        att_ref[:, 384 + i * 128:384 + (i + 1) * 128] = dq[i * 32:(i + 1) * 32]
+
+
+def attention_kernel(mask_ref, q_ref, do_ref, wide_ref, kv_ref, att_ref, dq_ref, dkv_ref, wide_out, s_ref, list_ref,
+                     count_ref):
     position = lax.axis_index("ctx")
     dkv_ref[...] = jnp.zeros_like(dkv_ref)
     for r in range(2):
+        for b in range(WIDEST):
+            list_ref[r, b] = 0
+
         def note(j, n):
             list_ref[r, n] = j
             return n + mask_ref[position * 2 + r, j]
         count_ref[r] = lax.fori_loop(0, 32, note, 0)
 
-    def unit(u, carry):
-        r, h = u // 4, u % 4
+    wide_row(wide_ref, kv_ref, wide_out, dkv_ref, s_ref, position // 4)
+
+    def unit(r, h):
+        n = count_ref[r]
         rows = pl.ds(pl.multiple_of(r * 128, 128), 128)
         cols = [pl.ds(pl.multiple_of(h * 384 + i * 128, 128), 128) for i in range(3)]
         kcol = pl.ds(pl.multiple_of(h * 128, 128), 128)
         vcol = pl.ds(pl.multiple_of(512 + h * 128, 128), 128)
         q = jnp.concatenate([q_ref[rows, c] for c in cols], axis=0)
         do = jnp.concatenate([do_ref[rows, c] for c in cols], axis=0)
-        n = count_ref[r]
-        pairs = (n + 1) // 2
-
-        def ids(p):
-            second = jnp.minimum(2 * p + 1, n - 1)
-            return list_ref[r, 2 * p], list_ref[r, second], 2 * p + 1 < n
-
-        def load(p, col):
-            a, b, _ = ids(p)
-            return jnp.concatenate([kv_ref[pl.ds(pl.multiple_of(a * 128, 128), 128), col],
-                                    kv_ref[pl.ds(pl.multiple_of(b * 128, 128), 128), col]], axis=0)
-
-        def score(p, m):
-            _, _, valid = ids(p)
-            s = lax.dot_general(load(p, kcol), q, (((1,), (1,)), ((), ())), preferred_element_type=jnp.float32) * scale
-            low = s[128:]
-            low = jnp.where(valid, low, -1e30)
-            s_ref[p, :128] = s[:128]
-            s_ref[p, 128:] = low
-            return jnp.maximum(m, jnp.maximum(jnp.max(s[:128], axis=0, keepdims=True), jnp.max(low, axis=0, keepdims=True)))
-        m = lax.fori_loop(0, pairs, score, jnp.full((1, 384), -1e30, jnp.float32))
-
-        def weigh(p, carry):
-            total, acc = carry
-            _, _, valid = ids(p)
-            e = jnp.exp(s_ref[p] - m)
-            s_ref[p] = e
-            total = total + jnp.sum(e, axis=0, keepdims=True)
-            acc = acc + lax.dot_general(load(p, vcol), e.astype(jnp.bfloat16), (((0,), (0,)), ((), ())), preferred_element_type=jnp.float32)
-            return total, acc
-        total, acc = lax.fori_loop(0, pairs, weigh, (jnp.zeros((1, 384), jnp.float32), jnp.zeros((128, 384), jnp.float32)))
-        inverse = 1.0 / total
-        out_t = acc * inverse
-        out = out_t.T
+        places = [pl.ds(pl.multiple_of(list_ref[r, b] * 128, 128), 128) for b in range(WIDEST)]
+        k = jnp.concatenate([kv_ref[w, kcol] for w in places], axis=0)
+        v = jnp.concatenate([kv_ref[w, vcol] for w in places], axis=0)
+        s = dot_nt(k, q) * FACTOR
+        s = jnp.concatenate([s[:256]] + [jnp.where(b < n, s[b * 128:(b + 1) * 128], -1e30)
+                                         for b in range(2, WIDEST)], axis=0)
+        dprob = dot_nt(v, do)
+        e = jnp.exp2(s - jnp.max(s, axis=0, keepdims=True))
+        half = e.astype(jnp.bfloat16)
+        inverse = 1.0 / jnp.sum(e, axis=0, keepdims=True)
+        out_t = dot_tn(v, half) * inverse
+        out = out_t.T.astype(jnp.bfloat16)
         for i in range(3):
-            att_ref[rows, cols[i]] = out[i * 128:(i + 1) * 128].astype(jnp.bfloat16)
-        out_half = out_t.astype(jnp.bfloat16).astype(jnp.float32)
-        do_t = do.astype(jnp.float32).T
-        delta = jnp.sum(out_half * do_t, axis=0, keepdims=True)
-
-        def back(p, dq_t):
-            a, b, valid = ids(p)
-            k, v = load(p, kcol), load(p, vcol)
-            prob = s_ref[p] * inverse
-            dprob = lax.dot_general(v, do, (((1,), (1,)), ((), ())), preferred_element_type=jnp.float32)
-            ds = (prob * (dprob - delta)).astype(jnp.bfloat16)
-            dv = jnp.dot(prob.astype(jnp.bfloat16), do, preferred_element_type=jnp.float32)
-            dk = jnp.dot(ds, q, preferred_element_type=jnp.float32) * scale
-            dq_t = dq_t + lax.dot_general(k, ds, (((0,), (0,)), ((), ())), preferred_element_type=jnp.float32)
-
-            def put(block, lo):
-                where = pl.ds(pl.multiple_of(block * 128, 128), 128)
-                dkv_ref[where, kcol] = (dkv_ref[where, kcol].astype(jnp.float32) + dk[lo:lo + 128]).astype(jnp.bfloat16)
-                dkv_ref[where, vcol] = (dkv_ref[where, vcol].astype(jnp.float32) + dv[lo:lo + 128]).astype(jnp.bfloat16)
-            put(a, 0)
-            pl.when(valid)(lambda: put(b, 128))
-            return dq_t
-        dq = lax.fori_loop(0, pairs, back, jnp.zeros((128, 384), jnp.float32)).T * scale
+            att_ref[rows, cols[i]] = out[i * 128:(i + 1) * 128]
+        delta = jnp.sum(out_t.astype(jnp.bfloat16).astype(jnp.float32) * do.astype(jnp.float32).T, axis=0,
+                        keepdims=True)
+        share = jnp.broadcast_to(inverse, (128, 384)).T
+        do_share = (do.astype(jnp.float32) * share).astype(jnp.bfloat16)
+        q_share = (q.astype(jnp.float32) * (share * SCALE)).astype(jnp.bfloat16)
+        ds = (e * (dprob - delta)).astype(jnp.bfloat16)
+        dv = dot_nn(half, do_share)
+        dk = dot_nn(ds, q_share)
+        dq = (dot_tn(k, ds) * (inverse * SCALE)).T.astype(jnp.bfloat16)
         for i in range(3):
-            dq_ref[rows, cols[i]] = dq[i * 128:(i + 1) * 128].astype(jnp.bfloat16)
-        return carry
-    lax.fori_loop(0, 8, unit, 0)
-
-def attention(block_mask, q, do, kv):
+            dq_ref[rows, cols[i]] = dq[i * 128:(i + 1) * 128]
+        for b, w in enumerate(places):
+            piece = slice(b * 128, (b + 1) * 128)
+            dkv_ref[w, kcol] = (dkv_ref[w, kcol].astype(jnp.float32) + dk[piece]).astype(jnp.bfloat16)
+            dkv_ref[w, vcol] = (dkv_ref[w, vcol].astype(jnp.float32) + dv[piece]).astype(jnp.bfloat16)
+
+    @pl.loop(0, 2)
+    def _(r):
+        @pl.when(count_ref[r] <= WIDEST)
+        def _():
+            @pl.loop(0, 4)
+            def _(h):
+                unit(r, h)
+
+        @pl.when(count_ref[r] > WIDEST)
+        def _():
+            rows = pl.ds(pl.multiple_of(r * 128, 128), 128)
+            att_ref[rows, :] = jnp.zeros((128, 1536), jnp.bfloat16)
+            dq_ref[rows, :] = jnp.zeros((128, 1536), jnp.bfloat16)
+
+
+def attention(block_mask, q, do, wide, kv):
     vm = pl.BlockSpec(memory_space=pltpu.VMEM)
+    half = jnp.bfloat16
     return pl.pallas_call(
         attention_kernel,
-        out_shape=(jax.ShapeDtypeStruct((256, 1536), jnp.bfloat16), jax.ShapeDtypeStruct((256, 1536), jnp.bfloat16),
-                   jax.ShapeDtypeStruct((4096, 1024), jnp.bfloat16)),
-        in_specs=[pl.BlockSpec(memory_space=pltpu.SMEM), vm, vm, vm],
-        out_specs=(vm, vm, vm),
-        scratch_shapes=[pltpu.VMEM((16, 256, 384), jnp.float32), pltpu.SMEM((2, 33), jnp.int32), pltpu.SMEM((2,), jnp.int32)],
+        out_shape=(jax.ShapeDtypeStruct((256, 1536), half), jax.ShapeDtypeStruct((256, 1536), half),
+                   jax.ShapeDtypeStruct((4096, 1024), half), jax.ShapeDtypeStruct((32, 768), half)),
+        in_specs=[pl.BlockSpec(memory_space=pltpu.SMEM), vm, vm, vm, vm],
+        out_specs=(vm, vm, vm, vm),
+        scratch_shapes=[pltpu.VMEM((4096, 128), jnp.float32), pltpu.SMEM((2, 33), jnp.int32),
+                        pltpu.SMEM((2,), jnp.int32)],
         compiler_params=pltpu.CompilerParams(vmem_limit_bytes=60 << 20),
         name="attention",
-    )(block_mask, q, do, kv)
-
-
-def grads_kernel(tok_ref, gain_ref, dq_ref, terms, w_all, out_ref, w_vm, mine, part, ahead, behind, after, before,
-                 relay, crossed, total, send_sem, recv_sem, local_sem):
+    )(block_mask, q, do, wide, kv)
+
+
+def grads_kernel(tok_ref, gain_ref, mask_ref, part_dq, part_att, wide_ref, terms, w_all, out_ref, att_ref, w_vm, mine,
+                 part, ahead, behind, after, before, relay, crossed, total, dq_ref, wide_box, send_sem, recv_sem,
+                 local_sem):
     p = Place()
     net = Net(send_sem, recv_sem)
     greet(p)
     order = [(dz, dy) for dz in (2, 0) for dy in (2, 1, 3, 0)]
     swap, up, down, north, south = p.ids(swap=True), p.ids(dz=1), p.ids(dz=-1), p.ids(dy=1), p.ids(dy=-1)
     loads = {}
+    for d in range(1, 16):
+        net.send("w%d" % d, wide_ref, wide_box.at[p.i], p.mate(d))
     for slot, (dz, dy) in enumerate(order):
         who, _ = p.ids(dy=dy, dz=dz)
         other, _ = p.ids(dy=dy, dz=dz, swap=True)
@@ -402,6 +491,19 @@
         net.recv("g%d" % plane)
         add(mine.at[base + 3], after.at[plane], before.at[plane])
 
+    def join():
+        wide_box[p.i] = wide_ref[...]
+        for d in range(1, 16):
+            net.recv("w%d" % d)
+        flags = [chosen(mask_ref, p, r) for r in range(2)]
+        for j in range(16):
+            cols = slice((j // 4) * 384, (j // 4 + 1) * 384)
+            for r in range(2):
+                rows = slice(r * 128 + (j % 4) * 32, r * 128 + (j % 4 + 1) * 32)
+                for out, local, lo in ((att_ref, part_att, 0), (dq_ref, part_dq, 384)):
+                    value = wide_box[j, :, lo:lo + 384].astype(jnp.float32) * flags[r]
+                    out[rows, cols] = (local[rows, cols].astype(jnp.float32) + value).astype(jnp.bfloat16)
+
     def query_part(first, last):
         @pl.loop(first, last)
         def _(t):
@@ -413,6 +515,7 @@
     far(4, 1)
     near(0, 0)
     near(4, 1)
+    join()
     weight.wait()
     query_part(0, 12)
     gathered(0, 0)
@@ -444,31 +547,32 @@
     net.drain()
 
 
-def input_grads(tokens, gain, dq, terms, weight):
+def input_grads(tokens, gain, mask, dq, att, wide, terms, weight):
     vm, anywhere = pl.BlockSpec(memory_space=pltpu.VMEM), pl.BlockSpec(memory_space=pl.ANY)
     half = jnp.bfloat16
     return pl.pallas_call(
         grads_kernel,
-        out_shape=jax.ShapeDtypeStruct((256, 3072), half),
-        in_specs=[vm, vm, vm, anywhere, anywhere],
-        out_specs=vm,
+        out_shape=(jax.ShapeDtypeStruct((256, 3072), half), jax.ShapeDtypeStruct((256, 1536), half)),
+        in_specs=[vm, vm, vm, vm, vm, vm, anywhere, anywhere],
+        out_specs=(vm, vm),
         scratch_shapes=[pltpu.VMEM((3072, 2560), half), pltpu.VMEM((8, 256, 1024), half),
                         pltpu.VMEM((8, 256, 1024), half), pltpu.VMEM((2, 128, 1024), half),
                         pltpu.VMEM((2, 128, 1024), half), pltpu.VMEM((2, 256, 1024), half),
                         pltpu.VMEM((2, 256, 1024), half), pltpu.VMEM((2, 128, 1024), half),
                         pltpu.VMEM((256, 1024), half), pltpu.VMEM((256, 3072), jnp.float32),
-                        pltpu.SemaphoreType.DMA((24,)), pltpu.SemaphoreType.DMA((24,)),
+                        pltpu.VMEM((256, 1536), half), pltpu.VMEM((16, 32, 768), half),
+                        pltpu.SemaphoreType.DMA((40,)), pltpu.SemaphoreType.DMA((40,)),
                         pltpu.SemaphoreType.DMA((9,))],
         compiler_params=pltpu.CompilerParams(vmem_limit_bytes=60 << 20, collective_id=1, has_side_effects=True),
         name="input_grads",
-    )(tokens, gain, dq, terms, weight)
+    )(tokens, gain, mask, dq, att, wide, terms, weight)
 
 
 def body(tokens, norm_gain, qkv_weight, block_mask, out_grad):
     gain = norm_gain[None]
-    queries, pairs_all, panels = project(tokens[0], gain, qkv_weight)
-    attended, query_grad, block_terms = attention(block_mask, queries, out_grad[0], pairs_all)
-    token_grad = input_grads(tokens[0], gain, query_grad, block_terms, panels)
+    queries, pairs_all, panels, wide = project(tokens[0], gain, block_mask, out_grad[0], qkv_weight)
+    part_att, part_dq, block_terms, wide_out = attention(block_mask, queries, out_grad[0], wide, pairs_all)
+    token_grad, attended = input_grads(tokens[0], gain, block_mask, part_dq, part_att, wide_out, block_terms, panels)
     return (attended[None], token_grad[None])
 
 

time: 229 us -> 193 us (0.84)
  Pallas kernels: 225 us -> 188 us
    pallas_call x1, Pallas kernels: 102 us -> 60.6 us  [input_grads(): pl.pallas_call(grads_kernel, out_shape=(jax.ShapeDtypeStruct((256, 3072),...]
    pallas_call x1, Pallas kernels: 93.5 us -> 102 us  [project(): pl.pallas_call(project_kernel, out_shape=(jax.ShapeDtypeStruct((256, 1536...]
    pallas_call x1, Pallas kernels: 29.6 us -> 25.2 us  [attention(): pl.pallas_call(attention_kernel, out_shape=(jax.ShapeDtypeStruct((256, 15...]
where the time goes in v4:
time: 193 us; the launch traced here: 192 us
  Pallas kernels  188 us (97%)
  local copies, waits for them, and re-layouts  3.33 us (2%)
    pallas_call x1, Pallas kernels, project(): pl.pallas_call(project_kernel, out_shape=(jax.ShapeDtypeStruct((256, 1536...  102 us
    pallas_call x1, Pallas kernels, input_grads(): pl.pallas_call(grads_kernel, out_shape=(jax.ShapeDtypeStruct((256, 3072),...  60.6 us
    pallas_call x1, Pallas kernels, attention(): pl.pallas_call(attention_kernel, out_shape=(jax.ShapeDtypeStruct((256, 15...  25.2 us

profile of v4, /device:TPU:0, one launch (start us, length us, event | category | flops | bytes accessed | tf_op | source)
XLA Modules:
  0.0 192.2 jit_solution(7945260374091021058)
XLA Ops:
  0.6 102.4 %project.1 = (bf16[256,1536]{1,0:T(8,128)(2,1)}, bf16[4096,1024]{1,0:T(8,128)(2,1)}, bf16[3072,2560]{1,0:T(8,128)(2,1)}, bf16[32,768]{1,0:T(8,128)(2,1)}) custom-call(bf16[256,3072]{1,0:T(8,128)(2,1)} %bitcast.5, f32[1,3072]{1,0:T(1,128)} %bitcast.11, s32[32,32]{1,0:T(8,128)} %mask_ref.5, bf16[256,1536]{1,0:T(8,128)(2,1)} %bitcast.7, bf16[384,2560]{1,0:T(8,128)(2,1)} %shard.1), custom_call_target="tpu_custom_call" | custom-call | tf_op jit(solution)/shard_map/project/pallas_call | solution.py:274
  103.0 25.2 %attention.1 = (bf16[256,1536]{1,0:T(8,128)(2,1)}, bf16[256,1536]{1,0:T(8,128)(2,1)}, bf16[4096,1024]{1,0:T(8,128)(2,1)}, bf16[32,768]{1,0:T(8,128)(2,1)}) custom-call(s32[32,32]{1,0:T(8,128)} %mask_ref.5, bf16[256,1536]{1,0:T(8,128)(2,1)} %get-tuple-element.12.q_ref, bf16[256,1536]{1,0:T(8,128)(2,1)} %bitcast.8, ...), custom_call_target="tpu_custom_call" | custom-call | tf_op jit(solution)/shard_map/attention/pallas_call | solution.py:426
  128.2 60.6 %input_grads.1 = (bf16[256,3072]{1,0:T(8,128)(2,1)}, bf16[256,1536]{1,0:T(8,128)(2,1)}) custom-call(bf16[256,3072]{1,0:T(8,128)(2,1)} %bitcast.6, f32[1,3072]{1,0:T(1,128)} %bitcast.12, s32[32,32]{1,0:T(8,128)} %mask_ref.5, bf16[256,1536]{1,0:T(8,128)(2,1)} %get-tuple-element.15.part_dq, bf16[256,1536]{1,0:T(8,128)(2,1)} %get-tuple-element.16.part_att, ...), custom_call_target="tpu_custom_call" | custom-call | tf_op jit(solution)/shard_map/input_grads/pallas_call | solution.py:553
  188.8 0.0 copy-start
  188.9 2.2 %copy.9 = bf16[1,256,1536]{2,1,0:T(8,128)(2,1)} copy(bf16[1,256,1536]{2,1,0:T(8,128)(2,1)} %bitcast.10) | data formatting | bytes 1572864
  191.0 0.0 copy-done
  191.0 1.1 copy.10
Async XLA Ops:
  188.8 2.2 %copy-start = (bf16[256,3072]{1,0:T(8,128)(2,1)S(1)}, bf16[256,3072]{1,0:T(8,128)(2,1)}, u32[]{:S(2)}) copy-start(bf16[256,3072]{1,0:T(8,128)(2,1)} %get-tuple-element.21) | copy-start | bytes 4718596

commit v5 on v4

--- a/solution.py
+++ b/solution.py
@@ -19,7 +19,9 @@
 
 MESH = pl.DeviceIdType.MESH
 D = 3072
-KEYS = pl.ds(1536, 1024)
+KEYS = pl.ds(1536, 512)
+VALUES = pl.ds(2048, 512)
+PAIRS = pl.ds(1536, 1024)
 QUERIES = pl.ds(0, 1536)
 
 
@@ -89,8 +91,9 @@
 
 
 class WeightGather:
-    def __init__(self, net, place, tag, shard, whole, cols):
+    def __init__(self, net, place, tag, shard, whole, cols, ring=False):
         self.net, self.p, self.tag, self.shard, self.whole, self.cols = net, place, tag, shard, whole, cols
+        self.ring = ring
 
     def at(self, dx, lo, count):
         shard_id = (self.p.f // 4) * 4 + (self.p.x + dx) % 4
@@ -99,9 +102,9 @@
     def own(self, lo, count):
         return self.shard.at[rows_at(self.p.c * 192 + lo, count), self.cols]
 
-    def cross(self, dx, lo):
+    def cross(self, dx, lo, count=96):
         shard_id = (1 - self.p.f // 4) * 4 + (self.p.x + dx) % 4
-        return self.whole.at[rows_at(shard_id * 384 + self.p.c * 192 + lo, 96), self.cols]
+        return self.whole.at[rows_at(shard_id * 384 + self.p.c * 192 + lo, count), self.cols]
 
     def put(self, name, piece, to, src=None):
         self.net.send(self.tag + name, piece if src is None else src, piece, to)
@@ -123,8 +126,9 @@
         self.got("x-")
         self.put("x-2", self.at(1, 96, 96), self.p.ids(dx=-1))
         for dx in (-1, 1):
-            self.put("z+%d" % dx, self.at(dx, 0, 96), self.p.ids(dz=1))
-            self.put("z-%d" % dx, self.at(dx, 96, 96), self.p.ids(dz=-1))
+            if not self.ring:
+                self.put("z+%d" % dx, self.at(dx, 0, 96), self.p.ids(dz=1))
+                self.put("z-%d" % dx, self.at(dx, 96, 96), self.p.ids(dz=-1))
             self.put("c%d" % dx, self.at(dx, 0, 192), self.p.ids(swap=True))
 
     def second(self):
@@ -133,18 +137,111 @@
             self.put("z%s2" % sign, self.at(2, lo, 96), self.p.ids(dz=dz))
             self.put("c2%s" % sign, self.at(2, lo, 96), self.p.ids(swap=True))
 
-    def third(self):
-        for dx in (0, -1, 1, 2):
+    def arrive(self, dxs):
+        for dx in dxs:
             for sign, lo in (("+", 0), ("-", 96)):
                 self.got("z%s%d" % (sign, dx))
                 self.put("cz%s%d" % (sign, dx), self.cross(dx, lo), self.p.ids(swap=True))
 
+    def spread(self):
+        for sign in (1, -1):
+            self.put("X%d" % sign, self.cross(0, 0, 192), self.p.ids(dx=sign))
+
+    def third(self):
+        if not self.ring:
+            self.arrive((0, -1, 1, 2))
+            return
+        self.arrive((2,))
+        for sign in (1, -1):
+            self.got("X%d" % sign)
+            self.put("cX%d" % sign, self.cross(-sign, 0, 192), self.p.ids(swap=True))
+
     def last(self):
         for name in ("c-1", "c1", "c2+", "c2-"):
             self.got(name)
-        for dx in (0, -1, 1, 2):
+        for dx in (0, 2) if self.ring else (0, -1, 1, 2):
             for sign in "+-":
                 self.got("cz%s%d" % (sign, dx))
+        if self.ring:
+            self.got("cX1")
+            self.got("cX-1")
+
+
+class BlockGather:
+    def __init__(self, net, place, tag, own, whole, relay, cols):
+        self.net, self.p, self.tag, self.mine, self.whole, self.relay, self.cols = net, place, tag, own, whole, relay, cols
+        p = place
+        self.swap, self.up, self.down = p.ids(swap=True), p.ids(dz=1), p.ids(dz=-1)
+        self.north, self.south = p.ids(dy=1), p.ids(dy=-1)
+        self.swapped = []
+
+    def home(self, dy=0, dz=0, lo=0, count=256):
+        who, _ = self.p.ids(dy=dy, dz=dz)
+        return self.whole.at[rows_at(who * 256 + lo, count), self.cols]
+
+    def own(self, lo=0, count=256):
+        return self.mine.at[pl.ds(lo, count), self.cols]
+
+    def put(self, name, piece, to, src=None):
+        self.net.send(self.tag + name, piece if src is None else src, piece, to)
+
+    def give(self, piece, src=None):
+        name = "c%d" % len(self.swapped)
+        self.put(name, piece, self.swap, src)
+        self.swapped.append(name)
+
+    def got(self, name):
+        self.net.recv(self.tag + name)
+
+    def start(self):
+        self.put("h+", self.relay.at[0, :, self.cols], self.up, self.own(0, 128))
+        self.put("h-", self.relay.at[1, :, self.cols], self.down, self.own(128, 128))
+        self.put("y+", self.home(), self.north, self.own())
+        self.put("y-", self.home(), self.south, self.own())
+        self.give(self.home(), self.own())
+
+    def relay_on(self):
+        self.got("h+")
+        self.put("r+", self.home(dz=-1, count=128), self.up, self.relay.at[0, :, self.cols])
+        self.got("h-")
+        self.put("r-", self.home(dz=1, lo=128, count=128), self.down, self.relay.at[1, :, self.cols])
+
+    def near(self):
+        self.got("y+")
+        self.put("y+2", self.home(dy=-1, count=128), self.north)
+        self.give(self.home(dy=-1))
+        self.got("y-")
+        self.put("y-2", self.home(dy=1, lo=128, count=128), self.south)
+        self.give(self.home(dy=1))
+
+    def cross(self):
+        for sign, lo in (("+", 0), ("-", 128)):
+            self.got("r" + sign)
+            piece = self.home(dz=2, lo=lo, count=128)
+            self.put("ty+" + sign, piece, self.north)
+            self.put("ty-" + sign, piece, self.south)
+            self.give(piece)
+
+    def far(self):
+        self.got("ty++")
+        self.put("ty+2", self.home(dy=-1, dz=2, count=128), self.north)
+        self.give(self.home(dy=-1, dz=2, count=128))
+        self.got("ty--")
+        self.put("ty-2", self.home(dy=1, dz=2, lo=128, count=128), self.south)
+        self.give(self.home(dy=1, dz=2, lo=128, count=128))
+        self.got("ty+-")
+        self.give(self.home(dy=-1, dz=2, lo=128, count=128))
+        self.got("ty-+")
+        self.give(self.home(dy=1, dz=2, count=128))
+
+    def tail(self):
+        for name, dz, lo in (("y+2", 0, 0), ("y-2", 0, 128), ("ty+2", 2, 0), ("ty-2", 2, 128)):
+            self.got(name)
+            self.give(self.home(dy=2, dz=dz, lo=lo, count=128))
+
+    def last(self):
+        for name in self.swapped:
+            self.got(name)
 
 
 def project_kernel(tok_ref, gain_ref, mask_ref, do_ref, shard, q_ref, kv_all, w_all, wide_ref, w_vm, normed, kv_own,
@@ -153,7 +250,10 @@
     net = Net(send_sem, recv_sem)
     greet(p)
     keys = WeightGather(net, p, "k", shard, w_vm, KEYS)
-    queries = WeightGather(net, p, "q", shard, w_vm, QUERIES)
+    values = WeightGather(net, p, "v", shard, w_vm, VALUES)
+    queries = WeightGather(net, p, "q", shard, w_vm, QUERIES, ring=True)
+    all_keys = BlockGather(net, p, "ak", kv_own, kv_all, relay, pl.ds(0, 512))
+    all_values = BlockGather(net, p, "av", kv_own, kv_all, relay, pl.ds(512, 512))
     keys.start_x()
     keys.start_z()
     mine = pltpu.make_async_copy(shard, w_vm.at[rows_at(p.f * 384, 384)], local_sem.at[0])
@@ -166,77 +266,58 @@
         inv_rms = lax.rsqrt(jnp.mean(x * x, axis=1, keepdims=True) + epsilon)
         normed[rows, :] = (x * inv_rms * gain_ref[...]).astype(jnp.bfloat16)
 
+    def pair_part(first, last):
+        @pl.loop(first, last)
+        def _(t):
+            cols = pl.ds(pl.multiple_of(t * 256, 256), 256)
+            part = jnp.dot(normed[...], w_vm[:, pl.ds(pl.multiple_of(1536 + t * 256, 256), 256)],
+                           preferred_element_type=jnp.float32)
+            kv_own[:, cols] = part.astype(jnp.bfloat16)
+
+    def exchange(name, box, pieces):
+        for d in range(1, 16):
+            net.send("%s%d" % (name, d), pieces.at[(p.i + d) % 16], box.at[d - 1], p.mate(d))
+
     cut(do_ref, mask_ref, p, do_cut)
     keys.first()
+    values.start_x()
+    keys.second()
+    values.start_z()
+    keys.third()
+    values.first()
     queries.start_x()
-    keys.second()
-    queries.start_z()
-    keys.third()
     keys.last()
     mine.wait()
-
-    @pl.loop(0, 4)
-    def _(t):
-        cols = pl.ds(pl.multiple_of(t * 256, 256), 256)
-        part = jnp.dot(normed[...], w_vm[:, pl.ds(pl.multiple_of(1536 + t * 256, 256), 256)],
-                       preferred_element_type=jnp.float32)
-        kv_own[:, cols] = part.astype(jnp.bfloat16)
-
-    keep_keys = pltpu.make_async_copy(w_vm.at[:, KEYS], w_all.at[:, KEYS], local_sem.at[1])
-    keep_keys.start()
-
-    def home(dy=0, dz=0, lo=0, count=256):
-        who, _ = p.ids(dy=dy, dz=dz)
-        return kv_all.at[rows_at(who * 256 + lo, count)]
-
-    def put(name, piece, to, src=None):
-        net.send(name, piece if src is None else src, piece, to)
-
-    swap, up, down, north, south = p.ids(swap=True), p.ids(dz=1), p.ids(dz=-1), p.ids(dy=1), p.ids(dy=-1)
-    put("y+", home(), north, kv_own)
-    put("y-", home(), south, kv_own)
-    put("h+", relay.at[0], up, kv_own.at[:128])
-    put("h-", relay.at[1], down, kv_own.at[128:])
-    put("cy0", home(), swap, kv_own)
-    stay = pltpu.make_async_copy(kv_own, home(), local_sem.at[2])
+    pair_part(0, 2)
+    all_keys.start()
+    values.second()
+    all_keys.relay_on()
+    queries.start_z()
+    all_keys.near()
+    values.third()
+    all_keys.cross()
+    values.last()
+    pair_part(2, 4)
+    all_values.start()
+    stay = pltpu.make_async_copy(kv_own, kv_all.at[rows_at(p.i * 256, 256)], local_sem.at[2])
     stay.start()
-
+    keep_pairs = pltpu.make_async_copy(w_vm.at[:, PAIRS], w_all.at[:, PAIRS], local_sem.at[1])
+    keep_pairs.start()
     queries.first()
-    net.recv("h+")
-    put("r+", home(dz=-1, count=128), up, relay.at[0])
-    net.recv("h-")
-    put("r-", home(dz=1, lo=128, count=128), down, relay.at[1])
+    all_values.relay_on()
+    queries.arrive((0,))
+    queries.spread()
+    all_keys.far()
     queries.second()
-    for sign, lo in (("+", 0), ("-", 128)):
-        net.recv("r" + sign)
-        piece = home(dz=2, lo=lo, count=128)
-        put("ty+" + sign, piece, north)
-        put("ty-" + sign, piece, south)
-        put("ct" + sign, piece, swap)
-    net.recv("y+")
-    put("y+2", home(dy=-1, count=128), north)
-    put("cy-", home(dy=-1), swap)
-    net.recv("y-")
-    put("y-2", home(dy=1, lo=128, count=128), south)
-    put("cy+", home(dy=1), swap)
+    all_values.near()
+    all_values.cross()
+    exchange("do", do_box, do_cut)
+    all_keys.tail()
     queries.third()
-    for d in range(1, 16):
-        put("do%d" % d, do_box.at[d - 1], p.mate(d), do_cut.at[(p.i + d) % 16])
     queries.last()
-
     keep_queries = pltpu.make_async_copy(w_vm.at[:, QUERIES], w_all.at[:, QUERIES], local_sem.at[3])
     keep_queries.start()
-
-    net.recv("ty++")
-    put("ty+2", home(dy=-1, dz=2, count=128), north)
-    put("ct-a", home(dy=-1, dz=2, count=128), swap)
-    net.recv("ty--")
-    put("ty-2", home(dy=1, dz=2, lo=128, count=128), south)
-    put("ct+b", home(dy=1, dz=2, lo=128, count=128), swap)
-    net.recv("ty+-")
-    put("ct-b", home(dy=-1, dz=2, lo=128, count=128), swap)
-    net.recv("ty-+")
-    put("ct+a", home(dy=1, dz=2, count=128), swap)
+    all_values.far()
 
     @pl.loop(0, 6)
     def _(t):
@@ -244,27 +325,18 @@
         q_ref[:, cols] = jnp.dot(normed[...], w_vm[:, cols], preferred_element_type=jnp.float32).astype(jnp.bfloat16)
 
     cut(q_ref, mask_ref, p, q_cut)
-    for d in range(1, 16):
-        put("qq%d" % d, q_box.at[d - 1], p.mate(d), q_cut.at[(p.i + d) % 16])
-
-    net.recv("y+2")
-    put("cy2a", home(dy=2, count=128), swap)
-    net.recv("y-2")
-    put("cy2b", home(dy=2, lo=128, count=128), swap)
-    net.recv("ty+2")
-    put("ct2a", home(dy=2, dz=2, count=128), swap)
-    net.recv("ty-2")
-    put("ct2b", home(dy=2, dz=2, lo=128, count=128), swap)
-    for name in ("cy0", "cy-", "cy+", "cy2a", "cy2b", "ct+", "ct-", "ct-a", "ct+b", "ct-b", "ct+a", "ct2a", "ct2b"):
-        net.recv(name)
-    for name, box, own, cols in (("qq", q_box, q_cut, slice(0, 384)), ("do", do_box, do_cut, slice(384, 768))):
+    exchange("qq", q_box, q_cut)
+    all_values.tail()
+    all_keys.last()
+    all_values.last()
+    for name, box, own, cols in (("do", do_box, do_cut, slice(384, 768)), ("qq", q_box, q_cut, slice(0, 384))):
         value = own[p.i]
         for d in range(1, 16):
             net.recv("%s%d" % (name, d))
             value = value + box[d - 1]
         wide_ref[:, cols] = value
     net.drain()
-    for copy in (stay, keep_keys, keep_queries):
+    for copy in (stay, keep_pairs, keep_queries):
         copy.wait()
 
 
@@ -280,8 +352,8 @@
         scratch_shapes=[pltpu.VMEM((3072, 2560), half), pltpu.VMEM((256, 3072), half), pltpu.VMEM((256, 1024), half),
                         pltpu.VMEM((2, 128, 1024), half), pltpu.VMEM((16, 32, 384), half),
                         pltpu.VMEM((16, 32, 384), half), pltpu.VMEM((15, 32, 384), half),
-                        pltpu.VMEM((15, 32, 384), half), pltpu.SemaphoreType.DMA((120,)),
-                        pltpu.SemaphoreType.DMA((120,)), pltpu.SemaphoreType.DMA((4,))],
+                        pltpu.VMEM((15, 32, 384), half), pltpu.SemaphoreType.DMA((160,)),
+                        pltpu.SemaphoreType.DMA((160,)), pltpu.SemaphoreType.DMA((4,))],
         compiler_params=pltpu.CompilerParams(vmem_limit_bytes=60 << 20, collective_id=0, has_side_effects=True),
         name="project",
     )(tokens, gain, mask, out_grad, shard)

time: 193 us -> 171 us (0.89)
  Pallas kernels: 188 us -> 165 us
    pallas_call x1, Pallas kernels: 102 us -> 79.8 us  [project(): pl.pallas_call(project_kernel, out_shape=(jax.ShapeDtypeStruct((256, 1536...]
where the time goes in v5:
time: 171 us; the launch traced here: 169 us
  Pallas kernels  165 us (96%)
  local copies, waits for them, and re-layouts  3.33 us (2%)
    pallas_call x1, Pallas kernels, project(): pl.pallas_call(project_kernel, out_shape=(jax.ShapeDtypeStruct((256, 1536...  79.8 us
    pallas_call x1, Pallas kernels, input_grads(): pl.pallas_call(grads_kernel, out_shape=(jax.ShapeDtypeStruct((256, 3072),...  60.4 us
    pallas_call x1, Pallas kernels, attention(): pl.pallas_call(attention_kernel, out_shape=(jax.ShapeDtypeStruct((256, 15...  25.2 us

profile of v5, /device:TPU:0, one launch (start us, length us, event | category | flops | bytes accessed | tf_op | source)
XLA Modules:
  0.0 169.4 jit_solution(7291684210197451783)
XLA Ops:
  0.6 79.8 %project.1 = (bf16[256,1536]{1,0:T(8,128)(2,1)}, bf16[4096,1024]{1,0:T(8,128)(2,1)}, bf16[3072,2560]{1,0:T(8,128)(2,1)}, bf16[32,768]{1,0:T(8,128)(2,1)}) custom-call(bf16[256,3072]{1,0:T(8,128)(2,1)} %bitcast.5, f32[1,3072]{1,0:T(1,128)} %bitcast.11, s32[32,32]{1,0:T(8,128)} %mask_ref.5, bf16[256,1536]{1,0:T(8,128)(2,1)} %bitcast.7, bf16[384,2560]{1,0:T(8,128)(2,1)} %shard.1), custom_call_target="tpu_custom_call" | custom-call | tf_op jit(solution)/shard_map/project/pallas_call | solution.py:346
  80.4 25.2 %attention.1 = (bf16[256,1536]{1,0:T(8,128)(2,1)}, bf16[256,1536]{1,0:T(8,128)(2,1)}, bf16[4096,1024]{1,0:T(8,128)(2,1)}, bf16[32,768]{1,0:T(8,128)(2,1)}) custom-call(s32[32,32]{1,0:T(8,128)} %mask_ref.5, bf16[256,1536]{1,0:T(8,128)(2,1)} %get-tuple-element.12.q_ref, bf16[256,1536]{1,0:T(8,128)(2,1)} %bitcast.8, ...), custom_call_target="tpu_custom_call" | custom-call | tf_op jit(solution)/shard_map/attention/pallas_call | solution.py:498
  105.7 60.4 %input_grads.1 = (bf16[256,3072]{1,0:T(8,128)(2,1)}, bf16[256,1536]{1,0:T(8,128)(2,1)}) custom-call(bf16[256,3072]{1,0:T(8,128)(2,1)} %bitcast.6, f32[1,3072]{1,0:T(1,128)} %bitcast.12, s32[32,32]{1,0:T(8,128)} %mask_ref.5, bf16[256,1536]{1,0:T(8,128)(2,1)} %get-tuple-element.15.part_dq, bf16[256,1536]{1,0:T(8,128)(2,1)} %get-tuple-element.16.part_att, ...), custom_call_target="tpu_custom_call" | custom-call | tf_op jit(solution)/shard_map/input_grads/pallas_call | solution.py:625
  166.1 0.0 copy-start
  166.1 2.2 %copy.9 = bf16[1,256,1536]{2,1,0:T(8,128)(2,1)} copy(bf16[1,256,1536]{2,1,0:T(8,128)(2,1)} %bitcast.10) | data formatting | bytes 1572864
  168.3 0.0 copy-done
  168.3 1.1 copy.10
Async XLA Ops:
  166.1 2.2 %copy-start = (bf16[256,3072]{1,0:T(8,128)(2,1)S(1)}, bf16[256,3072]{1,0:T(8,128)(2,1)}, u32[]{:S(2)}) copy-start(bf16[256,3072]{1,0:T(8,128)(2,1)} %get-tuple-element.21) | copy-start | bytes 4718596

commit v6 on v5

--- a/solution.py
+++ b/solution.py
@@ -517,8 +517,32 @@
     order = [(dz, dy) for dz in (2, 0) for dy in (2, 1, 3, 0)]
     swap, up, down, north, south = p.ids(swap=True), p.ids(dz=1), p.ids(dz=-1), p.ids(dy=1), p.ids(dy=-1)
     loads = {}
-    for d in range(1, 16):
-        net.send("w%d" % d, wide_ref, wide_box.at[p.i], p.mate(d))
+
+    def piece(dy, dz):
+        who, _ = p.ids(dy=dy, dz=dz)
+        return wide_box.at[who]
+
+    def forward(dz, hops):
+        for dy in hops:
+            src = wide_ref if dz == 0 else piece(0, 2)
+            net.send("w%d%d" % (dz, dy), src, piece(0, dz), p.ids(dy=dy))
+
+    def share():
+        net.send("wz", wide_ref, piece(0, 0), p.ids(dz=2))
+        forward(0, (1, 3, 2))
+        net.send("s00", wide_ref, piece(0, 0), swap)
+
+    def share_far():
+        net.recv("wz")
+        forward(2, (1, 3, 2))
+        net.send("s20", piece(0, 2), piece(0, 2), swap)
+
+    def hand_on():
+        for dz in (0, 2):
+            for dy in (1, 3, 2):
+                net.recv("w%d%d" % (dz, dy))
+                net.send("s%d%d" % (dz, dy), piece(-dy, dz), piece(-dy, dz), swap)
+
     for slot, (dz, dy) in enumerate(order):
         who, _ = p.ids(dy=dy, dz=dz)
         other, _ = p.ids(dy=dy, dz=dz, swap=True)
@@ -565,8 +589,9 @@
 
     def join():
         wide_box[p.i] = wide_ref[...]
-        for d in range(1, 16):
-            net.recv("w%d" % d)
+        for dz in (0, 2):
+            for dy in range(4):
+                net.recv("s%d%d" % (dz, dy))
         flags = [chosen(mask_ref, p, r) for r in range(2)]
         for j in range(16):
             cols = slice((j // 4) * 384, (j // 4 + 1) * 384)
@@ -585,18 +610,21 @@
 
     far(0, 0)
     far(4, 1)
+    share()
     near(0, 0)
+    share_far()
     near(4, 1)
-    join()
     weight.wait()
-    query_part(0, 12)
     gathered(0, 0)
     net.send("h+", mine.at[3, :128], relay.at[0], up)
     net.send("h-", mine.at[3, 128:], relay.at[1], down)
+    hand_on()
     net.recv("h+")
     net.send("r+", relay.at[0], crossed.at[:128], up)
     net.recv("h-")
     net.send("r-", relay.at[1], crossed.at[128:], down)
+    join()
+    query_part(0, 12)
     gathered(4, 1)
     net.recv("r+")
     net.recv("r-")

time: 171 us -> 166 us (0.971)
  Pallas kernels: 165 us -> 161 us
    pallas_call x1, Pallas kernels: 60.4 us -> 56.4 us  [input_grads(): pl.pallas_call(grads_kernel, out_shape=(jax.ShapeDtypeStruct((256, 3072),...]
where the time goes in v6:
time: 166 us; the launch traced here: 165 us
  Pallas kernels  161 us (97%)
  local copies, waits for them, and re-layouts  3.33 us (2%)
    pallas_call x1, Pallas kernels, project(): pl.pallas_call(project_kernel, out_shape=(jax.ShapeDtypeStruct((256, 1536...  79.8 us
    pallas_call x1, Pallas kernels, input_grads(): pl.pallas_call(grads_kernel, out_shape=(jax.ShapeDtypeStruct((256, 3072),...  56.4 us
    pallas_call x1, Pallas kernels, attention(): pl.pallas_call(attention_kernel, out_shape=(jax.ShapeDtypeStruct((256, 15...  25.2 us
    unnamed x4, local copies, waits for them, and re-layouts  3.33 us

profile of v6, /device:TPU:0, one launch (start us, length us, event | category | flops | bytes accessed | tf_op | source)
XLA Modules:
  0.0 165.4 jit_solution(14846873018840663634)
XLA Ops:
  0.6 79.8 %project.1 = (bf16[256,1536]{1,0:T(8,128)(2,1)}, bf16[4096,1024]{1,0:T(8,128)(2,1)}, bf16[3072,2560]{1,0:T(8,128)(2,1)}, bf16[32,768]{1,0:T(8,128)(2,1)}) custom-call(bf16[256,3072]{1,0:T(8,128)(2,1)} %bitcast.5, f32[1,3072]{1,0:T(1,128)} %bitcast.11, s32[32,32]{1,0:T(8,128)} %mask_ref.5, bf16[256,1536]{1,0:T(8,128)(2,1)} %bitcast.7, bf16[384,2560]{1,0:T(8,128)(2,1)} %shard.1), custom_call_target="tpu_custom_call" | custom-call | tf_op jit(solution)/shard_map/project/pallas_call | solution.py:346
  80.4 25.2 %attention.1 = (bf16[256,1536]{1,0:T(8,128)(2,1)}, bf16[256,1536]{1,0:T(8,128)(2,1)}, bf16[4096,1024]{1,0:T(8,128)(2,1)}, bf16[32,768]{1,0:T(8,128)(2,1)}) custom-call(s32[32,32]{1,0:T(8,128)} %mask_ref.5, bf16[256,1536]{1,0:T(8,128)(2,1)} %get-tuple-element.12.q_ref, bf16[256,1536]{1,0:T(8,128)(2,1)} %bitcast.8, ...), custom_call_target="tpu_custom_call" | custom-call | tf_op jit(solution)/shard_map/attention/pallas_call | solution.py:498
  105.7 56.4 %input_grads.1 = (bf16[256,3072]{1,0:T(8,128)(2,1)}, bf16[256,1536]{1,0:T(8,128)(2,1)}) custom-call(bf16[256,3072]{1,0:T(8,128)(2,1)} %bitcast.6, f32[1,3072]{1,0:T(1,128)} %bitcast.12, s32[32,32]{1,0:T(8,128)} %mask_ref.5, bf16[256,1536]{1,0:T(8,128)(2,1)} %get-tuple-element.15.part_dq, bf16[256,1536]{1,0:T(8,128)(2,1)} %get-tuple-element.16.part_att, ...), custom_call_target="tpu_custom_call" | custom-call | tf_op jit(solution)/shard_map/input_grads/pallas_call | solution.py:653
  162.1 0.0 copy-start
  162.1 2.2 %copy.9 = bf16[1,256,1536]{2,1,0:T(8,128)(2,1)} copy(bf16[1,256,1536]{2,1,0:T(8,128)(2,1)} %bitcast.10) | data formatting | bytes 1572864
  164.2 0.0 copy-done
  164.2 1.1 copy.10
Async XLA Ops:
  162.1 2.2 %copy-start = (bf16[256,3072]{1,0:T(8,128)(2,1)S(1)}, bf16[256,3072]{1,0:T(8,128)(2,1)}, u32[]{:S(2)}) copy-start(bf16[256,3072]{1,0:T(8,128)(2,1)} %get-tuple-element.21) | copy-start | bytes 4718596
